TPU v7x, 128 devices: a whole 4x4x4 slice. The times are simulated.
128 devices in a mesh: gx: 4 (over z_lo, core), gy: 8 (over x, z_hi), gz: 4 (over y).
Axes of the slice: x: 4, y: 4, z: 4 (z_hi: 2, z_lo: 2; z = z_hi * 2 + z_lo), core: 2. Of those that a mesh axis runs over, the one named last changes fastest.
Arguments:
- factor: bfloat16 [4096, 4096], P(None, ('gx', 'gy')), may hold values from -1 to 1, as said below
- kriging: bfloat16 [768, 4096], replicated, may hold values from -0.75 to 0.75
- normals: bfloat16 [4, 8, 4, 8, 8, 4096], P('gx', 'gy', 'gz'), may hold values from -6 to 6
- visit_order: int32 [4, 8, 4, 8], P('gx', 'gy', 'gz'), may hold values from 0 to 7, each once within a row
Outputs:
- evolved: float32 [8, 16, 8, 8, 4096], P('gx', 'gy', 'gz')
Inputs may be any that keep to these rules, and one draw needn't show every extreme that they name: `visit_order`: each device block's 8 entries name each of its draws once. `factor`: zero below the diagonal; diagonal entries between 0.5 and 1.
All inputs are finite; a program needn't handle non-finite values.
Results may differ from a plain program's by a relative error of at most 0.013.
Values may be sent and summed in bfloat16 or wider, within the bound.
No kernel may reach another device: no remote copies, remote signals or barrier semaphores. Data moves between devices by JAX's collectives and lax.ppermute only.
A program may use at most 128 MiB of HBM per device.

v0:
```python
import functools

import jax
import jax.numpy as jnp
import numpy as np
from jax import lax
from jax.experimental import pallas as pl
from jax.experimental.pallas import tpu as pltpu
from jax.sharding import PartitionSpec as P


TILE = 16
CELLS = 4096
FACE = 256
BX = 2
BY = 2
BZ = 2
TILES = 8
ENS = 8
N_GX = 4
N_GY = 8
N_GZ = 4
SPAN_X = N_GX * BX
SPAN_Y = N_GY * BY
SPAN_Z = N_GZ * BZ
LEVELS = SPAN_X + SPAN_Y + SPAN_Z - 2
COLS_DEV = CELLS // (N_GX * N_GY)
PART = COLS_DEV // N_GZ
HALF = PART // 2
STATE = 3 * FACE
PLANES = STATE // 128
FACE_COLS = 352
PARTS = 8
SLOTS = SPAN_Y + SPAN_X - 1 + SPAN_Z - 1 + 14

BF = jnp.bfloat16
F32 = jnp.float32


def column_orders():
    orders = []
    for s in range(N_GZ):
        z_cells = [(4 * e + (s + 1) % 4) * TILE + TILE - 1 for e in range(2)]
        y_cells = [7 * TILE + 4 * ((s - 15) % 4) + m for m in range(4)]
        first = z_cells + [c for c in y_cells if c not in z_cells]
        part = [c for c in range(COLS_DEV) if (c // TILE + c % TILE // 4) % 4 == s]
        orders.append(first + [c for c in part if c not in first])
    return np.array(orders, np.int32)


ORDERS = column_orders()


def state_order():
    rows = np.zeros(STATE, np.int32)
    cells = np.zeros(STATE, np.int32)
    for f in range(STATE):
        plane, lane = divmod(f, 128)
        if plane < 4:
            s, slot = plane, lane % 64
            if lane < 64:
                i, q = 30 + slot // 32, slot % 32
                v, w = 8 * (i % 2) + ORDERS[s, q] // TILE, ORDERS[s, q] % TILE
                rows[f], cells[f] = v * 16 + w, (15 * 16 + v) * 16 + w
            else:
                u, w = slot // 4, 4 * ((s - 15) % 4) + slot % 4
                rows[f], cells[f] = FACE + u * 16 + w, (u * 16 + 15) * 16 + w
        else:
            s, slot = 2 * (plane - 4) + lane // 64, lane % 64
            i, e = slot // 2, slot % 2
            u, v = i // 2, 8 * (i % 2) + 4 * e + (s + 1) % 4
            rows[f], cells[f] = 2 * FACE + u * 16 + v, (u * 16 + v) * 16 + 15
    return rows, cells


STATE_ROWS, STATE_CELLS = state_order()


def one_hot(condition):
    return condition.astype(BF)


def iota(shape, axis):
    return lax.broadcasted_iota(jnp.int32, shape, axis)


def to_bf16_dot(left, right):
    return jnp.dot(left, right, preferred_element_type=F32).astype(BF)


def plane_shift(value, dx, dz, swap=0):
    pairs = []
    for gx in range(N_GX):
        for gy in range(N_GY):
            x, z, core = gy // 2, (gy % 2) * 2 + gx // 2, gx % 2
            move_x, move_z = (dx, dz) if core == 0 else (dz, dx)
            x, z, core = (x + move_x) % 4, (z + move_z) % 4, core ^ swap
            pairs.append((gx * N_GY + gy, ((z % 2) * 2 + core) * N_GY + x * 2 + z // 2))
    return lax.ppermute(value, ("gx", "gy"), pairs)


def line_shift(value, steps):
    return lax.ppermute(value, "gz", [(s, (s + steps) % N_GZ) for s in range(N_GZ)])


def slot_of(d):
    return d % 2 * 2 + d // 2


def by_core(core, refs, body):
    own, other = refs[:4], refs[4:]

    @pl.when(core == 0)
    def _():
        body(own, other)

    @pl.when(core == 1)
    def _():
        body(other, own)


def noise_kernel(place, *refs):
    row_refs = refs[:4]
    piece_refs = refs[4:12]
    noise_out = refs[12]
    rows, factors, acc, sem_rows, sem_factor = refs[13:]
    x, z, core = place[0], place[1], place[2]
    for back in range(N_GZ):
        pltpu.make_async_copy(row_refs[back], rows.at[back], sem_rows).start()

    def load_all(first_refs, second_refs):
        for parity in range(2):
            group = lax.rem(z + parity, 2)
            for dz in (parity, parity + 2):
                high = lax.rem(z - dz + 4, 4) // 2
                for dx in range(4):
                    target = (lax.rem(x - dx + 4, 4) * 2 + high) * 4
                    for t in range(2):
                        for ref, slot, kind in (
                            (first_refs[dz], slot_of(dx), 0),
                            (second_refs[dx], slot_of(dz), 2),
                        ):
                            pltpu.make_async_copy(
                                ref.at[pl.ds(t * 64 + slot * 16, 16)],
                                factors.at[group, target + kind + t],
                                sem_factor.at[parity],
                            ).start()

    by_core(core, piece_refs, load_all)
    pltpu.make_async_copy(rows, rows, sem_rows).wait()
    wide = 512
    for parity in range(2):
        group = lax.rem(z + parity, 2)
        block = factors.at[group]
        pltpu.make_async_copy(block, block, sem_factor.at[parity]).wait()
        acc[...] = jnp.zeros_like(acc)

        @pl.loop(0, 2 * group + 2)
        def _(chunk):
            span = pl.ds(pl.multiple_of(chunk * 1024, 1024), 1024)
            acc[...] += lax.dot_general(
                rows[:, :, span].reshape(N_GZ * 64, 1024),
                factors[group, :, :, span].reshape(wide, 1024),
                (((1,), (1,)), ((), ())),
                preferred_element_type=F32,
            )

        noise_out[:, pl.ds(pl.multiple_of(group * wide, wide), wide)] = acc[...].astype(BF)


def face_kernel(place, select, row_order, *refs):
    row_refs = refs[:4]
    piece_refs = refs[4:12]
    copies_out = refs[12]
    rows, factors, face_out, sem_rows, sem_factor, sem_out = refs[13:]
    x, z, core = place[0], place[1], place[2]
    odd = lax.rem(z + 1, 2)
    holder = lax.rem(x + 1, 4)

    def load(chunk, ref, start, target, count):
        span = pl.ds(chunk * 1024, 1024)
        pltpu.make_async_copy(
            ref.at[pl.ds(start, count), span],
            factors.at[chunk, pl.ds(target, count)],
            sem_factor.at[chunk],
        ).start()

    def load_rows(chunk):
        for back in range(N_GZ):
            pltpu.make_async_copy(
                row_refs[back].at[:, pl.ds(chunk * 1024, 1024)],
                rows.at[chunk, back],
                sem_rows.at[chunk],
            ).start()

    def load_all(first_refs, second_refs):
        for chunk in range(4):
            load_rows(chunk)
            load_chunk(functools.partial(load, chunk), first_refs, second_refs)

    def load_chunk(load, first_refs, second_refs):
        for dz in range(4):
            load(first_refs[dz], 0, 96 + dz * 64, 64)
        held = pl.multiple_of(64 + slot_of(holder) * 16, 16)
        part = pl.multiple_of(odd * 32, 32)
        for parity in range(2):

            @pl.when(odd == parity)
            def _():
                load(first_refs[parity], held, 0, 16)
                load(first_refs[parity + 2], held, 16, 16)

        for dx in range(4):

            @pl.when(holder == dx)
            def _():
                load(second_refs[dx], part, 32, 32)
                load(second_refs[dx], part + 64, 64, 32)

    by_core(core, piece_refs, load_all)
    product = jnp.zeros((N_GZ * 64, FACE_COLS), F32)
    for chunk in range(4):
        row_block, factor_block = rows.at[chunk], factors.at[chunk]
        pltpu.make_async_copy(row_block, row_block, sem_rows.at[chunk]).wait()
        pltpu.make_async_copy(factor_block, factor_block, sem_factor.at[chunk]).wait()
        product += lax.dot_general(
            rows[chunk].reshape(N_GZ * 64, 1024),
            factors[chunk],
            (((1,), (1,)), ((), ())),
            preferred_element_type=F32,
        )
    product = product.astype(BF)
    sums = jnp.dot(product, select[...], preferred_element_type=F32).astype(BF)
    faces = jnp.dot(row_order[...], sums, preferred_element_type=F32)
    low = iota((8, 128), 1) < 64
    for r in range(ENS):
        for a in range(BX):
            base = r * 32 + a * 16
            face_out[a, r, 0:16, :] = faces[base : base + 16, :128].astype(BF)
            first = faces[base : base + 8, 128:]
            second = faces[base + 8 : base + 16, 128:]
            face_out[a, r, 16:24, :] = jnp.where(low, first, second).astype(BF)
    copies = [
        pltpu.make_async_copy(face_out, copies_out.at[side, :, :, k], sem_out.at[side * N_GZ + k])
        for side in range(N_GX // 2)
        for k in range(N_GZ)
    ]
    for copy in copies:
        copy.start()
    for copy in copies:
        copy.wait()


def sweep_kernel(place, own_ref, other_ref, step_ref, reorder_ref, out, *scratch):
    noise, history, state, picked, own_half, other_half, step, reorder, sems = scratch
    core, gz = place[2], place[3]
    gx = lax.rem(place[1], 2) * 2 + core
    low8 = iota((8, 128), 1) < 64
    count = N_GY * N_GZ
    for bx in range(N_GX):
        chunk = pl.ds(bx * count, count)
        pltpu.make_async_copy(own_ref.at[chunk], own_half.at[chunk], sems.at[2 * bx]).start()
        pltpu.make_async_copy(other_ref.at[chunk], other_half.at[chunk], sems.at[2 * bx + 1]).start()
    load_step = pltpu.make_async_copy(step_ref, step, sems.at[8])
    load_reorder = pltpu.make_async_copy(reorder_ref, reorder, sems.at[9])
    load_step.start()
    load_reorder.start()

    for p in range(PLANES):
        for i in range(SPAN_X):
            noise[p, i * SLOTS * 8 : (i * SLOTS + 14) * 8, :] = jnp.zeros((112, 128), F32)

    def place_block(bx, by):
        block = bx * N_GY + by
        for a, half in ((core, own_half), (1 - core, other_half)):
            planes = [half[block * N_GZ + s, 0:16, :].astype(F32) for s in range(N_GZ)]
            zs = [half[block * N_GZ + s, 16:24, :].astype(F32) for s in range(N_GZ)]
            for b in range(BY):
                start = ((bx * BX + a) * SLOTS + by * BY + b + 14) * 8
                start = pl.multiple_of(start, 8)
                for p in range(4):
                    noise[p, pl.ds(start, 8), :] = planes[p][b * 8 : (b + 1) * 8]
                for pair in range(2):
                    first, second = zs[2 * pair], zs[2 * pair + 1]
                    if b == 0:
                        second = pltpu.roll(second, 64, 1)
                    else:
                        first = pltpu.roll(first, 64, 1)
                    noise[4 + pair, pl.ds(start, 8), :] = jnp.where(low8, first, second)

    for bx in range(N_GX):
        chunk = pl.ds(bx * count, count)
        pltpu.make_async_copy(own_ref.at[chunk], own_half.at[chunk], sems.at[2 * bx]).wait()
        pltpu.make_async_copy(other_ref.at[chunk], other_half.at[chunk], sems.at[2 * bx + 1]).wait()

        @pl.loop(0, N_GY)
        def _(by):
            place_block(bx, by)

    state[...] = jnp.zeros_like(state)
    low = iota((64, 128), 1) < 64
    has_below = (iota((64, 128), 0) % 8) != 7
    load_step.wait()

    @pl.loop(0, LEVELS, unroll=3)
    def _(level):
        upstream = []
        for p in range(PLANES):
            here = state[p]
            if p < 4:
                west = jnp.concatenate([jnp.zeros((8, 128), F32), here[:56]], 0)
                value = jnp.where(low, west, here)
            else:
                value = jnp.where(has_below, pltpu.roll(here, 63, 0), 0.0)
            history[p, pl.ds(pl.multiple_of(level * 64, 64), 64), :] = value
            upstream.append(value.astype(BF))
        joined = jnp.concatenate(upstream, 1)
        first = jnp.dot(joined, step[:, :256], preferred_element_type=F32)
        second = jnp.dot(joined, step[:, 256:512], preferred_element_type=F32)
        third = jnp.dot(joined[:, :384], step[:384, 512:], preferred_element_type=F32)
        third += jnp.dot(joined[:, 384:], step[384:, 512:], preferred_element_type=F32)
        result = jnp.concatenate([first, second, third], 1)
        for p in range(PLANES):
            rows = []
            for i in range(SPAN_X):
                start = (i * SLOTS + level - i + 7) * 8
                rows.append(noise[p, pl.ds(start, 8, stride=9), :])
            state[p] = result[:, p * 128 : (p + 1) * 128] + jnp.concatenate(rows, 0)

    for a in range(BX):
        for b in range(BY):
            for c in range(BZ):
                i = gx * BX + a
                k = gz * BZ + c
                start = (i + k + b) * 64 + i * 8 + 7 - k
                for p in range(PLANES):
                    picked[p, pl.ds((a * BY + b) * BZ + c, 8, stride=8), :] = history[
                        p, pl.ds(start, 8, stride=128), :
                    ]
    load_reorder.wait()
    values = jnp.concatenate([picked[p].astype(BF) for p in range(PLANES)], 1)
    out[...] = jnp.dot(values, reorder[...], preferred_element_type=F32).astype(BF)


def natural_kernel(place, first, second, third, fourth, spread, out):
    gz = place[3]
    total = jnp.zeros((512, 512), F32)
    for back, part in enumerate((first, second, third, fourth)):
        source = lax.rem(gz + back, N_GZ)
        stacked = jnp.concatenate([part[:, g * 128 : (g + 1) * 128] for g in range(8)], 0)
        total += jnp.dot(stacked, spread[source], preferred_element_type=F32)
    for g in range(8):
        for c in range(2):
            start = (g // 4 * 2 + c) * 1024 + g % 4 * 256
            values = total[g * 64 : (g + 1) * 64, c * 256 : (c + 1) * 256]
            out[:, start : start + 256] = values.astype(BF)


def final_kernel(faces, swap_rows, kriging, noise, out, weights, values, loads, stores):
    width = CELLS // PARTS
    copies = []
    for g in range(PARTS):
        source = kriging.at[:, pl.ds(g * width, width)]
        copies.append(pltpu.make_async_copy(source, weights.at[g], loads.at[g]))
        copies[g].start()
    upstream = jnp.dot(swap_rows[...], faces[...], preferred_element_type=F32).astype(BF)
    results = []
    for g in range(PARTS):
        span = slice(g * width, (g + 1) * width)
        copies[g].wait()
        product = jnp.dot(upstream, weights[g], preferred_element_type=F32)
        values[g] = product + noise[:, span].astype(F32)
        results.append(pltpu.make_async_copy(values.at[g], out.at[:, span], stores.at[g]))
        results[g].start()
    for result in results:
        result.wait()


def select_table():
    table = np.full((N_GX, N_GY, N_GZ, 3, FACE_COLS), -1, np.int32)
    for gx in range(N_GX):
        for gy in range(N_GY):
            x, z = gy // 2, (gy % 2) * 2 + gx // 2
            parity = (z + 1) % 2
            for s in range(N_GZ):
                lanes = table[gx, gy, s]
                for j in range(2):
                    start = (z - parity - 2 * j) % 4 // 2 * 32
                    for r in range(8):
                        lanes[0, j * 16 + 8 + r] = start + 8 + r
                        lanes[0, 32 + j * 16 + 8 + r] = start + 16 + r
                        lanes[0, 64 + j * 16 + 8 + r] = start + 24 + r
                for dz in range(4):
                    for dx in range(4):
                        for sc in range(2):
                            sx, sz = (x - dx) % 4, (z - dz) % 4
                            i = ((sz % 2) * 2 + sc) * N_GY + sx * 2 + sz // 2
                            base = 96 + dz * 64 + slot_of(dx) * 16 + sc * 8
                            for r in range(8):
                                column = ORDERS[s, r]
                                if i >= 30:
                                    lanes[0, base + r] = (i - 30) * 32 + r
                                if i % 2 == 1 and column // TILE == 7:
                                    lanes[1, base + r] = 64 + (i // 2) * 4 + column % 4
                                if r < 2:
                                    lanes[2, base + r] = 128 + i * 2 + r
    return table.reshape(-1, 3 * FACE_COLS)


def row_table():
    order = np.zeros((N_GZ, 256), np.int32)
    for gz in range(N_GZ):
        for target in range(256):
            k = 7 - target % 8
            tile = (target // 8 % 4) * 2 + k % 2
            order[gz, target] = ((gz - k // 2) % N_GZ) * 64 + tile * 8 + target // 32
    return order


def spread_table():
    table = np.zeros((N_GZ, 128), np.int32)
    for s in range(N_GZ):
        for n in range(128):
            device, q, core = n // 64, n % 64 // 16 * 8 + n % 8, n % 16 // 8
            table[s, n] = core * 256 + device * COLS_DEV + ORDERS[s, q]
    return table


def own_table():
    swapped = np.concatenate([ORDERS[:, HALF:], ORDERS[:, :HALF]], 1)
    return np.stack([ORDERS, swapped], 1).reshape(-1, PART)


def local(factor, kriging, normals, visit_order):
    gx = lax.axis_index("gx")
    gy = lax.axis_index("gy")
    gz = lax.axis_index("gz")
    place = jnp.stack([gy // 2, (gy % 2) * 2 + gx // 2, gx % 2, gz]).astype(jnp.int32)
    vmem = pl.BlockSpec(memory_space=pltpu.VMEM)
    smem = pl.BlockSpec(memory_space=pltpu.SMEM)
    anywhere = pl.BlockSpec(memory_space=pl.ANY)

    core = gx % 2
    own_columns = jnp.asarray(own_table())[gz * 2 + core]
    own = one_hot(iota((PART, COLS_DEV), 1) == own_columns[:, None])
    shard = lax.dot_general(
        own, factor, (((1,), (1,)), ((), ())), preferred_element_type=F32
    ).astype(BF)
    mine = shard[:HALF].reshape(2, 8, CELLS)
    given = plane_shift(shard[HALF:], 0, 0, 1).reshape(2, 8, CELLS)
    is_first = core == 0
    both = jnp.concatenate([jnp.where(is_first, mine, given), jnp.where(is_first, given, mine)], 1)
    line = [both]
    for d in (1, 2, 3):
        line.append(plane_shift(both, d, 0))
    line = jnp.concatenate([line[d] for d in (0, 2, 1, 3)], 1).reshape(8 * HALF, CELLS)

    drawn = normals.reshape(TILES, ENS, CELLS)
    ordered = drawn.at[visit_order.reshape(TILES)].get(mode="promise_in_bounds")
    ordered = ordered.reshape(TILES * ENS, CELLS)
    row_pieces = [ordered]
    for s in (1, 2, 3):
        row_pieces.append(line_shift(ordered, s))

    late, kriging_late, line, spread_places, state_rows = lax.optimization_barrier(
        (gz, kriging, line, jnp.asarray(spread_table()), jnp.asarray(STATE_ROWS))
    )
    lane = iota((FACE_COLS, 256), 1)
    device = (gx * N_GY + gy) * N_GZ + late
    lanes = jnp.asarray(select_table())[device].reshape(3, FACE_COLS, 1)
    select = one_hot(
        (lane == lanes[0]) | (lane == lanes[1]) | (lane == lanes[2])
        | ((lane - 64 == lanes[2]) & (lane >= 192))
    )
    row_order = one_hot(iota((256, 256), 1) == jnp.asarray(row_table())[late][:, None])
    spread = one_hot(iota((N_GZ, 128, 512), 2) == spread_places[:, :, None])
    reorder = one_hot(state_rows[:, None] == iota((STATE, STATE), 1))
    swap_rows = one_hot(
        iota((64, 64), 1) == jnp.asarray([(r % 8) * 8 + r // 8 for r in range(64)])[:, None]
    )
    to_state = one_hot(iota((CELLS, STATE), 0) == jnp.asarray(STATE_CELLS)[None, :])
    step = to_bf16_dot(reorder, to_bf16_dot(kriging_late, to_state))

    held = [line]
    for d in (1, 2, 3):
        held.append(plane_shift(line, 0, d))
    held[1], select, row_order, spread, step, reorder, place = lax.optimization_barrier(
        (held[1], select, row_order, spread, step, reorder, place)
    )
    pieces = held + [plane_shift(line, 0, 0, 1)]
    pieces += [plane_shift(piece, 0, 0, 1) for piece in held[1:]]

    copies = pl.pallas_call(
        face_kernel,
        out_shape=jax.ShapeDtypeStruct((N_GX // 2, BX, ENS, N_GZ, 24, 128), BF),
        in_specs=[smem, vmem, vmem] + [anywhere] * 12,
        out_specs=anywhere,
        scratch_shapes=[
            pltpu.VMEM((4, N_GZ, 64, 1024), BF),
            pltpu.VMEM((4, FACE_COLS, 1024), BF),
            pltpu.VMEM((BX, ENS, 24, 128), BF),
            pltpu.SemaphoreType.DMA((4,)),
            pltpu.SemaphoreType.DMA((4,)),
            pltpu.SemaphoreType.DMA((N_GX // 2 * N_GZ,)),
        ],
        compiler_params=pltpu.CompilerParams(vmem_limit_bytes=16 << 20),
        name="face_part",
    )(place, select, row_order, *row_pieces, *pieces)

    place, copies = lax.optimization_barrier((place, copies))
    noise_part = pl.pallas_call(
        noise_kernel,
        out_shape=jax.ShapeDtypeStruct((N_GZ * 64, N_GX * N_GY * PART), BF),
        in_specs=[smem] + [anywhere] * 12,
        out_specs=vmem,
        scratch_shapes=[
            pltpu.VMEM((N_GZ, 64, CELLS), BF),
            pltpu.VMEM((2, 32, 16, CELLS), BF),
            pltpu.VMEM((256, 512), F32),
            pltpu.SemaphoreType.DMA,
            pltpu.SemaphoreType.DMA((2,)),
        ],
        name="noise_part",
    )(place, *row_pieces, *pieces)

    received = lax.all_to_all(copies.reshape(128, 24, 128), ("gx", "gy", "gz"), 0, 0, tiled=True)
    parts = [noise_part[back * 64 : (back + 1) * 64] for back in range(N_GZ)]
    home = [parts[0]]
    for back in (1, 2, 3):
        home.append(line_shift(parts[back], -back))
    other_half = plane_shift(received, 0, 0, 1)

    chosen = pl.pallas_call(
        sweep_kernel,
        out_shape=jax.ShapeDtypeStruct((64, STATE), BF),
        in_specs=[smem] + [anywhere] * 4,
        out_specs=vmem,
        scratch_shapes=[
            pltpu.VMEM((PLANES, SPAN_X * SLOTS * 8, 128), F32),
            pltpu.VMEM((PLANES, LEVELS * 64, 128), F32),
            pltpu.VMEM((PLANES, 64, 128), F32),
            pltpu.VMEM((PLANES, 64, 128), F32),
            pltpu.VMEM((128, 24, 128), BF),
            pltpu.VMEM((128, 24, 128), BF),
            pltpu.VMEM((STATE, STATE), BF),
            pltpu.VMEM((STATE, STATE), BF),
            pltpu.SemaphoreType.DMA((10,)),
        ],
        name="sweep",
    )(place, received, other_half, step, reorder)

    upstream = lax.all_to_all(
        chosen.reshape(N_GY, TILES, STATE), "gy", 0, 0, tiled=True
    ).reshape(ENS * TILES, STATE)

    natural = pl.pallas_call(
        natural_kernel,
        out_shape=jax.ShapeDtypeStruct((TILES * ENS, CELLS), BF),
        in_specs=[smem] + [vmem] * 5,
        out_specs=vmem,
        name="natural",
    )(place, *home, spread)

    out = pl.pallas_call(
        final_kernel,
        out_shape=jax.ShapeDtypeStruct((TILES * ENS, CELLS), F32),
        in_specs=[vmem, vmem, anywhere, vmem],
        out_specs=anywhere,
        scratch_shapes=[
            pltpu.VMEM((PARTS, STATE, CELLS // PARTS), BF),
            pltpu.VMEM((PARTS, TILES * ENS, CELLS // PARTS), F32),
            pltpu.SemaphoreType.DMA((PARTS,)),
            pltpu.SemaphoreType.DMA((PARTS,)),
        ],
        name="evolve",
    )(upstream, swap_rows, kriging, natural)
    return out.reshape(BX, BY, BZ, ENS, CELLS)


def solution(mesh):
    placed = (
        P(None, ("gx", "gy")),
        P(),
        P("gx", "gy", "gz", None, None, None),
        P("gx", "gy", "gz", None),
    )

    return jax.shard_map(
        local,
        mesh=mesh,
        in_specs=placed,
        out_specs=P("gx", "gy", "gz", None, None),
        check_vma=False,
    )
```

profile of v0, /device:TPU:16, one launch (start us, length us, event | category | flops | bytes accessed | tf_op | source)
XLA Modules:
  0.0 137.9 jit_solution(7462237610536863387)
XLA Ops:
  0.0 0.8 fusion.15
  0.8 0.5 copy-done
  1.2 0.5 convolution_convert_fusion
  1.7 0.0 copy-start.19
  1.8 0.1 collective-permute-start
  1.9 0.7 fusion.16
  2.5 1.6 %gather_fusion = bf16[8,8,4096]{2,1,0:T(8,128)(2,1)S(1)} fusion(bf16[8,8,4096]{2,1,0:T(8,128)(2,1)} %bitcast.38, s32[1024]{0:T(1024)S(1)} %pad_clamp_fusion), kind=kCustom, calls=%fused_computation | custom fusion | bytes 1048608 | tf_op jit(solution)/shard_map/gather | solution.py:459
  4.2 1.4 collective-permute-start.5
  5.5 0.6 collective-permute-start.6
  6.1 0.0 collective-permute-done
  6.3 3.1 %collective-permute-start.1 = (bf16[2,16,4096]{2,1,0:T(8,128)(2,1)S(1)}, bf16[2,16,4096]{2,1,0:T(8,128)(2,1)}, u32[]{:S(2)}, u32[]{:S(2)}) collective-permute-start(bf16[2,16,4096]{2,1,0:T(8,128)(2,1)S(1)} %pad_maximum_fusion), channel_id=1, source_target_pairs={{0,16},{4,20},{8,24},{12,28},{16,0},{20,4},{24,8},{28,12},{32,36},... | collective-permute-start | bytes 786440 | tf_op jit(solution)/shard_map/ppermute | solution.py:99
  9.4 0.1 pad_add_fusion.place
  9.4 0.6 collective-permute-start.2
  10.1 2.6 %collective-permute-start.3 = (bf16[2,16,4096]{2,1,0:T(8,128)(2,1)S(1)}, bf16[2,16,4096]{2,1,0:T(8,128)(2,1)S(1)}, u32[]{:S(2)}, u32[]{:S(2)}) collective-permute-start(bf16[2,16,4096]{2,1,0:T(8,128)(2,1)S(1)} %pad_maximum_fusion), channel_id=1, source_target_pairs={{0,24},{4,28},{8,0},{12,4},{16,8},{20,12},{24,16},{28,20},{32,100}... | collective-permute-start | bytes 786440 | tf_op jit(solution)/shard_map/ppermute | solution.py:99
  12.7 1.6 %collective-permute-done.1 = bf16[2,16,4096]{2,1,0:T(8,128)(2,1)} collective-permute-done((bf16[2,16,4096]{2,1,0:T(8,128)(2,1)S(1)}, bf16[2,16,4096]{2,1,0:T(8,128)(2,1)}, u32[]{:S(2)}, u32[]{:S(2)}) %collective-permute-start.1) | collective-permute-done | bytes 262176 | tf_op jit(solution)/shard_map/ppermute | solution.py:99
  14.3 1.0 constant_dynamic-update-slice_fusion.2
  15.3 1.8 %collective-permute-done.2 = bf16[2,16,4096]{2,1,0:T(8,128)(2,1)S(1)} collective-permute-done((bf16[2,16,4096]{2,1,0:T(8,128)(2,1)S(1)}, bf16[2,16,4096]{2,1,0:T(8,128)(2,1)S(1)}, u32[]{:S(2)}, u32[]{:S(2)}) %collective-permute-start.2) | collective-permute-done | bytes 262176 | tf_op jit(solution)/shard_map/ppermute | solution.py:99
  17.1 0.0 collective-permute-done.3
  17.1 0.0 copy-start.1
  17.1 2.0 %collective-permute-start.4 = (bf16[128,4096]{1,0:T(8,128)(2,1)S(1)}, bf16[128,4096]{1,0:T(8,128)(2,1)}, u32[]{:S(2)}, u32[]{:S(2)}) collective-permute-start(bf16[128,4096]{1,0:T(8,128)(2,1)S(1)} %bitcast.26), channel_id=1, source_target_pairs={{0,64},{4,68},{8,72},{12,76},{16,80},{20,84},{24,88},{28,92},{32,4... | collective-permute-start | bytes 3145736 | tf_op jit(solution)/shard_map/ppermute | solution.py:99
  19.1 3.6 %collective-permute-start.8 = (bf16[128,4096]{1,0:T(8,128)(2,1)S(1)}, bf16[128,4096]{1,0:T(8,128)(2,1)}, u32[]{:S(2)}, u32[]{:S(2)}) collective-permute-start(bf16[128,4096]{1,0:T(8,128)(2,1)S(1)} %bitcast.27), channel_id=1, source_target_pairs={{0,4},{4,0},{8,12},{12,8},{16,20},{20,16},{24,28},{28,24},{32,48},... | collective-permute-start | bytes 3145736 | tf_op jit(solution)/shard_map/ppermute | solution.py:99
  22.7 1.0 collective-permute-start.9
  23.7 10.6 %fusion.4.step_ref = bf16[768,768]{1,0:T(8,128)(2,1)} fusion(s32[768]{0:T(1024)S(1)} %copy-done.16, bf16[768,4096]{1,0:T(8,128)(2,1)} %kriging.1, s32[768]{0:T(1024)S(1)} %copy-done.19), kind=kOutput, calls=%fused_computation.8 | convolution fusion | flops 5742723072 | bytes 7477248 | tf_op jit(solution)/shard_map/dot_general | solution.py:88
  34.3 0.9 dynamic-slice_reduce_fusion
  35.2 0.7 constant_dynamic-slice_fusion
  35.9 0.2 fusion.11.select
  36.1 0.1 fusion.12.row_order
  36.2 1.0 fusion.7.spread
  37.2 1.3 fusion.2.reorder_ref
  38.5 0.0 collective-permute-done.4.refs_5_
  38.5 0.0 collective-permute-start.10
  38.5 0.0 collective-permute-done.5.refs_1_
  38.5 0.5 collective-permute-start.11
  39.0 7.8 %collective-permute-done.8.refs_6_ = bf16[128,4096]{1,0:T(8,128)(2,1)} collective-permute-done((bf16[128,4096]{1,0:T(8,128)(2,1)S(1)}, bf16[128,4096]{1,0:T(8,128)(2,1)}, u32[]{:S(2)}, u32[]{:S(2)}) %collective-permute-start.8) | collective-permute-done | bytes 1048608 | tf_op jit(solution)/shard_map/ppermute | solution.py:99
  46.8 0.0 collective-permute-start.12
  46.8 0.0 collective-permute-done.9.refs_7_
  46.8 0.5 collective-permute-start.13
  47.3 0.0 collective-permute-done.6.refs_2_
  47.3 1.1 collective-permute-start.7
  48.4 13.3 %collective-permute-done.7.refs_3_ = bf16[64,4096]{1,0:T(8,128)(2,1)S(1)} collective-permute-done((bf16[64,4096]{1,0:T(8,128)(2,1)S(1)}, bf16[64,4096]{1,0:T(8,128)(2,1)S(1)}, u32[]{:S(2)}, u32[]{:S(2)}) %collective-permute-start.7) | collective-permute-done | bytes 524320 | tf_op jit(solution)/shard_map/ppermute | solution.py:103
  61.7 0.0 collective-permute-done.10.refs_8_
  61.7 0.0 collective-permute-done.11.refs_9_
  61.7 0.0 collective-permute-done.12.refs_10_
  61.8 4.9 %face_part.1 = bf16[2,2,8,4,24,128]{5,4,3,2,1,0:T(8,128)(2,1)S(1)} custom-call(s32[4]{0:T(128)S(1)} %pad_add_fusion.place, bf16[352,256]{1,0:T(8,128)(2,1)S(1)} %fusion.11.select, bf16[256,256]{1,0:T(8,128)(2,1)S(1)} %fusion.12.row_order, bf16[64,4096]{1,0:T(8,128)(2,1)S(1)} %bitcast.35, bf16[64,4096]{1,0:T(8,128)(2,1)S(1)} %collective-permute-done.5.refs_1_, ...), custom_call_target="tpu_custom_call" | custom-call | tf_op jit(solution)/shard_map/face_part/pallas_call | solution.py:493
  66.8 23.8 %all_to_all.10.own_ref = bf16[128,24,128]{2,1,0:T(8,128)(2,1)S(1)} all-to-all(bf16[128,24,128]{2,1,0:T(8,128)(2,1)S(1)} %bitcast.37), channel_id=1, replica_groups=mesh['gx'=4,'gy'=8,'gz'=4] {'gx','gy','gz'}, dimensions={0} | all-to-all | bytes 1572864 | tf_op jit(solution)/shard_map/all_to_all | solution.py:526
  90.6 0.8 collective-permute-start.14
  91.3 7.4 %noise_part.1 = bf16[256,1024]{1,0:T(8,128)(2,1)} custom-call(s32[4]{0:T(128)} %copy-done.9, bf16[64,4096]{1,0:T(8,128)(2,1)} %bitcast.36, bf16[64,4096]{1,0:T(8,128)(2,1)} %copy-done.7, bf16[64,4096]{1,0:T(8,128)(2,1)} %collective-permute-done.6.refs_2_, bf16[64,4096]{1,0:T(8,128)(2,1)} %copy-done.8, bf16[128,4096]{1,0:T(8,128)(2,1)} %bitcast.31, ...), custom_call_target="tpu_custom_call" | custom-call | tf_op jit(solution)/shard_map/noise_part/pallas_call | solution.py:511
  98.7 1.8 %fusion.17 = (bf16[64,1024]{1,0:T(8,128)(2,1)S(1)}, bf16[64,1024]{1,0:T(8,128)(2,1)S(1)}, bf16[64,1024]{1,0:T(8,128)(2,1)S(1)}, bf16[64,1024]{1,0:T(8,128)(2,1)}) fusion(bf16[256,1024]{1,0:T(8,128)(2,1)} %noise_part.1), kind=kLoop, calls=%fused_computation.46 | loop fusion | bytes 1048576 | tf_op jit(solution)/shard_map/slice | solution.py:527
  100.5 2.4 %collective-permute-start.15 = (bf16[64,1024]{1,0:T(8,128)(2,1)S(1)}, bf16[64,1024]{1,0:T(8,128)(2,1)S(1)}, u32[]{:S(2)}, u32[]{:S(2)}) collective-permute-start(bf16[64,1024]{1,0:T(8,128)(2,1)S(1)} %get-tuple-element.42), channel_id=1, source_target_pairs={{0,3},{1,0},{2,1},{3,2},{4,7},{5,4},{6,5},{7,6},{8,11},{9,8},{10,9... | collective-permute-start | bytes 393224 | tf_op jit(solution)/shard_map/ppermute | solution.py:103
  102.8 0.8 collective-permute-start.16
  103.7 2.6 %collective-permute-start.17 = (bf16[64,1024]{1,0:T(8,128)(2,1)S(1)}, bf16[64,1024]{1,0:T(8,128)(2,1)S(1)}, u32[]{:S(2)}, u32[]{:S(2)}) collective-permute-start(bf16[64,1024]{1,0:T(8,128)(2,1)S(1)} %get-tuple-element.40), channel_id=1, source_target_pairs={{0,1},{1,2},{2,3},{3,0},{4,5},{5,6},{6,7},{7,4},{8,9},{9,10},{10,1... | collective-permute-start | bytes 393224 | tf_op jit(solution)/shard_map/ppermute | solution.py:103
  106.3 0.0 collective-permute-done.14.other_ref
  106.3 0.9 copy-done.11
  107.2 13.7 %sweep.1 = bf16[64,768]{1,0:T(8,128)(2,1)} custom-call(s32[4]{0:T(128)} %copy-done.9, bf16[128,24,128]{2,1,0:T(8,128)(2,1)} %copy-done.10, bf16[128,24,128]{2,1,0:T(8,128)(2,1)} %copy-done.11, bf16[768,768]{1,0:T(8,128)(2,1)} %fusion.4.step_ref, bf16[768,768]{1,0:T(8,128)(2,1)} %fusion.2.reorder_ref), custom_call_target="tpu_custom_call" | custom-call | tf_op jit(solution)/shard_map/sweep/pallas_call | solution.py:533
  120.9 3.4 %all-to-all-start.1 = ((bf16[8,8,768]{2,1,0:T(8,128)(2,1)}), bf16[8,8,768]{2,1,0:T(8,128)(2,1)S(1)}, u32[]{:S(2)}, u32[]{:S(2)}) async-start(bf16[8,8,768]{2,1,0:T(8,128)(2,1)} %bitcast.40), calls=%async_computation.1 | async-start | bytes 196608 | tf_op jit(solution)/shard_map/all_to_all | solution.py:552
  124.3 0.7 fusion.13.swap_rows
  125.0 0.0 collective-permute-done.17.fourth
  125.0 0.6 copy-done.13
  125.6 0.0 copy-done.14
  125.7 0.0 copy-done.15
  125.7 2.8 %natural.1.noise = bf16[64,4096]{1,0:T(8,128)(2,1)} custom-call(s32[4]{0:T(128)} %copy-done.9, bf16[64,1024]{1,0:T(8,128)(2,1)} %get-tuple-element.43.first, bf16[64,1024]{1,0:T(8,128)(2,1)} %copy-done.13, bf16[64,1024]{1,0:T(8,128)(2,1)} %copy-done.14, bf16[64,1024]{1,0:T(8,128)(2,1)} %copy-done.15, bf16[4,128,512]{2,1,0:T(8,128)(2,1)} %fusion.7.spread), custom_call_target="tpu_custom_call" | custom-call | tf_op jit(solution)/shard_map/natural/pallas_call | solution.py:556
  128.5 3.5 %all-to-all-done.1 = bf16[8,8,768]{2,1,0:T(8,128)(2,1)S(1)} async-done(((bf16[8,8,768]{2,1,0:T(8,128)(2,1)}), bf16[8,8,768]{2,1,0:T(8,128)(2,1)S(1)}, u32[]{:S(2)}, u32[]{:S(2)}) %all-to-all-start.1) | async-done | bytes 98336 | tf_op jit(solution)/shard_map/all_to_all | solution.py:552
  132.0 0.6 copy-done.12
  132.7 5.1 %evolve.1 = f32[64,4096]{1,0:T(8,128)} custom-call(bf16[64,768]{1,0:T(8,128)(2,1)} %bitcast.39, bf16[64,64]{1,0:T(8,128)(2,1)} %fusion.13.swap_rows, bf16[768,4096]{1,0:T(8,128)(2,1)} %kriging.1, bf16[64,4096]{1,0:T(8,128)(2,1)} %natural.1.noise), custom_call_target="tpu_custom_call" | custom-call | tf_op jit(solution)/shard_map/evolve/pallas_call | solution.py:564
  (44 shorter events, 0.2 us)
Async XLA Ops:
  0.0 1.2 copy-start
  1.7 22.0 %copy-start.16 = (s32[768]{0:T(1024)S(1)}, s32[768]{0:T(1024)}, u32[]{:S(2)}) copy-start(s32[768]{0:T(1024)} %constant.80.clone) | copy-start | bytes 9220
  1.7 22.0 %copy-start.19 = (s32[768]{0:T(1024)S(1)}, s32[768]{0:T(1024)}, u32[]{:S(2)}) copy-start(s32[768]{0:T(1024)} %constant.84.clone) | copy-start | bytes 9220
  1.8 4.4 %collective-permute-start = (bf16[16,4096]{1,0:T(8,128)(2,1)S(1)}, bf16[16,4096]{1,0:T(8,128)(2,1)S(1)}, u32[]{:S(2)}, u32[]{:S(2)}) collective-permute-start(bf16[16,4096]{1,0:T(8,128)(2,1)S(1)} %slice.43), channel_id=1, source_target_pairs={{0,32},{4,36},{8,40},{12,44},{16,48},{20,52},{24,56},{28,60},{32,0... | collective-permute-start | bytes 393224 | tf_op jit(solution)/shard_map/ppermute | solution.py:99
  4.2 57.6 %copy-start.2 = (bf16[8,8,4096]{2,1,0:T(8,128)(2,1)}, bf16[8,8,4096]{2,1,0:T(8,128)(2,1)S(1)}, u32[]{:S(2)}) copy-start(bf16[8,8,4096]{2,1,0:T(8,128)(2,1)S(1)} %gather_fusion) | copy-start | bytes 1572868
  4.2 34.3 %collective-permute-start.5 = (bf16[64,4096]{1,0:T(8,128)(2,1)S(1)}, bf16[64,4096]{1,0:T(8,128)(2,1)S(1)}, u32[]{:S(2)}, u32[]{:S(2)}) collective-permute-start(bf16[64,4096]{1,0:T(8,128)(2,1)S(1)} %bitcast.32), channel_id=1, source_target_pairs={{0,1},{1,2},{2,3},{3,0},{4,5},{5,6},{6,7},{7,4},{8,9},{9,10},{10,1... | collective-permute-start | bytes 1572872 | tf_op jit(solution)/shard_map/ppermute | solution.py:103
  5.5 41.8 %collective-permute-start.6 = (bf16[64,4096]{1,0:T(8,128)(2,1)S(1)}, bf16[64,4096]{1,0:T(8,128)(2,1)}, u32[]{:S(2)}, u32[]{:S(2)}) collective-permute-start(bf16[64,4096]{1,0:T(8,128)(2,1)S(1)} %bitcast.33), channel_id=1, source_target_pairs={{0,2},{1,3},{2,0},{3,1},{4,6},{5,7},{6,4},{7,5},{8,10},{9,11},{10,... | collective-permute-start | bytes 1572872 | tf_op jit(solution)/shard_map/ppermute | solution.py:103
  6.3 8.1 %collective-permute-start.1 = (bf16[2,16,4096]{2,1,0:T(8,128)(2,1)S(1)}, bf16[2,16,4096]{2,1,0:T(8,128)(2,1)}, u32[]{:S(2)}, u32[]{:S(2)}) collective-permute-start(bf16[2,16,4096]{2,1,0:T(8,128)(2,1)S(1)} %pad_maximum_fusion), channel_id=1, source_target_pairs={{0,16},{4,20},{8,24},{12,28},{16,0},{20,4},{24,8},{28,12},{32,36},... | collective-permute-start | bytes 786440 | tf_op jit(solution)/shard_map/ppermute | solution.py:99
  9.4 52.3 %copy-start.9 = (s32[4]{0:T(128)}, s32[4]{0:T(128)S(1)}, u32[]{:S(2)}) copy-start(s32[4]{0:T(128)S(1)} %pad_add_fusion.place) | copy-start | bytes 52
  9.4 7.6 %collective-permute-start.2 = (bf16[2,16,4096]{2,1,0:T(8,128)(2,1)S(1)}, bf16[2,16,4096]{2,1,0:T(8,128)(2,1)S(1)}, u32[]{:S(2)}, u32[]{:S(2)}) collective-permute-start(bf16[2,16,4096]{2,1,0:T(8,128)(2,1)S(1)} %pad_maximum_fusion), channel_id=1, source_target_pairs={{0,8},{4,12},{8,16},{12,20},{16,24},{20,28},{24,0},{28,4},{32,96},... | collective-permute-start | bytes 786440 | tf_op jit(solution)/shard_map/ppermute | solution.py:99
  10.1 7.0 %collective-permute-start.3 = (bf16[2,16,4096]{2,1,0:T(8,128)(2,1)S(1)}, bf16[2,16,4096]{2,1,0:T(8,128)(2,1)S(1)}, u32[]{:S(2)}, u32[]{:S(2)}) collective-permute-start(bf16[2,16,4096]{2,1,0:T(8,128)(2,1)S(1)} %pad_maximum_fusion), channel_id=1, source_target_pairs={{0,24},{4,28},{8,0},{12,4},{16,8},{20,12},{24,16},{28,20},{32,100}... | collective-permute-start | bytes 786440 | tf_op jit(solution)/shard_map/ppermute | solution.py:99
  17.1 44.6 %copy-start.1 = (bf16[2,64,4096]{2,1,0:T(8,128)(2,1)}, bf16[2,64,4096]{2,1,0:T(8,128)(2,1)S(1)}, u32[]{:S(2)}) copy-start(bf16[2,64,4096]{2,1,0:T(8,128)(2,1)S(1)} %constant_dynamic-update-slice_fusion) | copy-start | bytes 3145732
  17.1 21.3 %collective-permute-start.4 = (bf16[128,4096]{1,0:T(8,128)(2,1)S(1)}, bf16[128,4096]{1,0:T(8,128)(2,1)}, u32[]{:S(2)}, u32[]{:S(2)}) collective-permute-start(bf16[128,4096]{1,0:T(8,128)(2,1)S(1)} %bitcast.26), channel_id=1, source_target_pairs={{0,64},{4,68},{8,72},{12,76},{16,80},{20,84},{24,88},{28,92},{32,4... | collective-permute-start | bytes 3145736 | tf_op jit(solution)/shard_map/ppermute | solution.py:99
  19.1 27.7 %collective-permute-start.8 = (bf16[128,4096]{1,0:T(8,128)(2,1)S(1)}, bf16[128,4096]{1,0:T(8,128)(2,1)}, u32[]{:S(2)}, u32[]{:S(2)}) collective-permute-start(bf16[128,4096]{1,0:T(8,128)(2,1)S(1)} %bitcast.27), channel_id=1, source_target_pairs={{0,4},{4,0},{8,12},{12,8},{16,20},{20,16},{24,28},{28,24},{32,48},... | collective-permute-start | bytes 3145736 | tf_op jit(solution)/shard_map/ppermute | solution.py:99
  22.7 24.1 %collective-permute-start.9 = (bf16[128,4096]{1,0:T(8,128)(2,1)S(1)}, bf16[128,4096]{1,0:T(8,128)(2,1)}, u32[]{:S(2)}, u32[]{:S(2)}) collective-permute-start(bf16[128,4096]{1,0:T(8,128)(2,1)S(1)} %bitcast.28), channel_id=1, source_target_pairs={{0,68},{4,64},{8,76},{12,72},{16,84},{20,80},{24,92},{28,88},{32,5... | collective-permute-start | bytes 3145736 | tf_op jit(solution)/shard_map/ppermute | solution.py:99
  23.7 12.5 %copy-start.17 = (s32[4,128]{1,0:T(4,128)S(1)}, s32[4,128]{1,0:T(4,128)}, u32[]{:S(2)}) copy-start(s32[4,128]{1,0:T(4,128)} %constant.79.clone) | copy-start | bytes 6148
  38.5 23.2 %collective-permute-start.10 = (bf16[128,4096]{1,0:T(8,128)(2,1)S(1)}, bf16[128,4096]{1,0:T(8,128)(2,1)S(1)}, u32[]{:S(2)}, u32[]{:S(2)}) collective-permute-start(bf16[128,4096]{1,0:T(8,128)(2,1)S(1)} %bitcast.29), channel_id=1, source_target_pairs={{0,32},{4,36},{8,40},{12,44},{16,48},{20,52},{24,56},{28,60},{32,0... | collective-permute-start | bytes 3145736 | tf_op jit(solution)/shard_map/ppermute | solution.py:99
  38.5 28.2 %copy-start.7 = (bf16[64,4096]{1,0:T(8,128)(2,1)}, bf16[64,4096]{1,0:T(8,128)(2,1)S(1)}, u32[]{:S(2)}) copy-start(bf16[64,4096]{1,0:T(8,128)(2,1)S(1)} %collective-permute-done.5.refs_1_) | copy-start | bytes 1572868
  38.5 23.2 %collective-permute-start.11 = (bf16[128,4096]{1,0:T(8,128)(2,1)}, bf16[128,4096]{1,0:T(8,128)(2,1)S(1)}, u32[]{:S(2)}, u32[]{:S(2)}) collective-permute-start(bf16[128,4096]{1,0:T(8,128)(2,1)} %collective-permute-done.4.refs_5_), channel_id=1, source_target_pairs={{0,32},{4,36},{8,40},{12,44},{16,48},{20,52},{24,56},{28,60},{32,0... | collective-permute-start | bytes 3145736 | tf_op jit(solution)/shard_map/ppermute | solution.py:99
  46.8 14.9 %collective-permute-start.12 = (bf16[128,4096]{1,0:T(8,128)(2,1)}, bf16[128,4096]{1,0:T(8,128)(2,1)S(1)}, u32[]{:S(2)}, u32[]{:S(2)}) collective-permute-start(bf16[128,4096]{1,0:T(8,128)(2,1)} %collective-permute-done.8.refs_6_), channel_id=1, source_target_pairs={{0,32},{4,36},{8,40},{12,44},{16,48},{20,52},{24,56},{28,60},{32,0... | collective-permute-start | bytes 3145736 | tf_op jit(solution)/shard_map/ppermute | solution.py:99
  46.8 14.9 %collective-permute-start.13 = (bf16[128,4096]{1,0:T(8,128)(2,1)}, bf16[128,4096]{1,0:T(8,128)(2,1)S(1)}, u32[]{:S(2)}, u32[]{:S(2)}) collective-permute-start(bf16[128,4096]{1,0:T(8,128)(2,1)} %collective-permute-done.9.refs_7_), channel_id=1, source_target_pairs={{0,32},{4,36},{8,40},{12,44},{16,48},{20,52},{24,56},{28,60},{32,0... | collective-permute-start | bytes 3145736 | tf_op jit(solution)/shard_map/ppermute | solution.py:99
  47.3 14.3 %collective-permute-start.7 = (bf16[64,4096]{1,0:T(8,128)(2,1)S(1)}, bf16[64,4096]{1,0:T(8,128)(2,1)S(1)}, u32[]{:S(2)}, u32[]{:S(2)}) collective-permute-start(bf16[64,4096]{1,0:T(8,128)(2,1)S(1)} %bitcast.34), channel_id=1, source_target_pairs={{0,3},{1,0},{2,1},{3,2},{4,7},{5,4},{6,5},{7,6},{8,11},{9,8},{10,9... | collective-permute-start | bytes 1572872 | tf_op jit(solution)/shard_map/ppermute | solution.py:103
  61.7 5.0 %copy-start.8 = (bf16[64,4096]{1,0:T(8,128)(2,1)}, bf16[64,4096]{1,0:T(8,128)(2,1)S(1)}, u32[]{:S(2)}) copy-start(bf16[64,4096]{1,0:T(8,128)(2,1)S(1)} %collective-permute-done.7.refs_3_) | copy-start | bytes 1572868
  61.7 5.0 %copy-start.3 = (bf16[128,4096]{1,0:T(8,128)(2,1)}, bf16[128,4096]{1,0:T(8,128)(2,1)S(1)}, u32[]{:S(2)}) copy-start(bf16[128,4096]{1,0:T(8,128)(2,1)S(1)} %collective-permute-done.10.refs_8_) | copy-start | bytes 3145732
  61.7 5.0 %copy-start.4 = (bf16[128,4096]{1,0:T(8,128)(2,1)}, bf16[128,4096]{1,0:T(8,128)(2,1)S(1)}, u32[]{:S(2)}) copy-start(bf16[128,4096]{1,0:T(8,128)(2,1)S(1)} %collective-permute-done.11.refs_9_) | copy-start | bytes 3145732
  61.7 5.0 %copy-start.5 = (bf16[128,4096]{1,0:T(8,128)(2,1)}, bf16[128,4096]{1,0:T(8,128)(2,1)S(1)}, u32[]{:S(2)}) copy-start(bf16[128,4096]{1,0:T(8,128)(2,1)S(1)} %collective-permute-done.12.refs_10_) | copy-start | bytes 3145732
  61.8 5.0 %copy-start.6 = (bf16[128,4096]{1,0:T(8,128)(2,1)}, bf16[128,4096]{1,0:T(8,128)(2,1)S(1)}, u32[]{:S(2)}) copy-start(bf16[128,4096]{1,0:T(8,128)(2,1)S(1)} %collective-permute-done.13.refs_11_) | copy-start | bytes 3145732
  90.6 8.1 %copy-start.10 = (bf16[128,24,128]{2,1,0:T(8,128)(2,1)}, bf16[128,24,128]{2,1,0:T(8,128)(2,1)S(1)}, u32[]{:S(2)}) copy-start(bf16[128,24,128]{2,1,0:T(8,128)(2,1)S(1)} %all_to_all.10.own_ref) | copy-start | bytes 2359300
  90.6 15.8 %collective-permute-start.14 = (bf16[128,24,128]{2,1,0:T(8,128)(2,1)S(1)}, bf16[128,24,128]{2,1,0:T(8,128)(2,1)S(1)}, u32[]{:S(2)}, u32[]{:S(2)}) collective-permute-start(bf16[128,24,128]{2,1,0:T(8,128)(2,1)S(1)} %all_to_all.10.own_ref), channel_id=1, source_target_pairs={{0,32},{4,36},{8,40},{12,44},{16,48},{20,52},{24,56},{28,60},{32,0... | collective-permute-start | bytes 2359304 | tf_op jit(solution)/shard_map/ppermute | solution.py:99
  100.5 23.8 %copy-start.18 = (s32[64]{0:T(128)S(1)}, s32[64]{0:T(128)}, u32[]{:S(2)}) copy-start(s32[64]{0:T(128)} %constant.83.clone) | copy-start | bytes 772
  100.5 24.5 %collective-permute-start.15 = (bf16[64,1024]{1,0:T(8,128)(2,1)S(1)}, bf16[64,1024]{1,0:T(8,128)(2,1)S(1)}, u32[]{:S(2)}, u32[]{:S(2)}) collective-permute-start(bf16[64,1024]{1,0:T(8,128)(2,1)S(1)} %get-tuple-element.42), channel_id=1, source_target_pairs={{0,3},{1,0},{2,1},{3,2},{4,7},{5,4},{6,5},{7,6},{8,11},{9,8},{10,9... | collective-permute-start | bytes 393224 | tf_op jit(solution)/shard_map/ppermute | solution.py:103
  102.8 22.1 %collective-permute-start.16 = (bf16[64,1024]{1,0:T(8,128)(2,1)S(1)}, bf16[64,1024]{1,0:T(8,128)(2,1)S(1)}, u32[]{:S(2)}, u32[]{:S(2)}) collective-permute-start(bf16[64,1024]{1,0:T(8,128)(2,1)S(1)} %get-tuple-element.41), channel_id=1, source_target_pairs={{0,2},{1,3},{2,0},{3,1},{4,6},{5,7},{6,4},{7,5},{8,10},{9,11},{10,... | collective-permute-start | bytes 393224 | tf_op jit(solution)/shard_map/ppermute | solution.py:103
  103.7 21.3 %collective-permute-start.17 = (bf16[64,1024]{1,0:T(8,128)(2,1)S(1)}, bf16[64,1024]{1,0:T(8,128)(2,1)S(1)}, u32[]{:S(2)}, u32[]{:S(2)}) collective-permute-start(bf16[64,1024]{1,0:T(8,128)(2,1)S(1)} %get-tuple-element.40), channel_id=1, source_target_pairs={{0,1},{1,2},{2,3},{3,0},{4,5},{5,6},{6,7},{7,4},{8,9},{9,10},{10,1... | collective-permute-start | bytes 393224 | tf_op jit(solution)/shard_map/ppermute | solution.py:103
  106.3 0.9 copy-start.11
  120.9 11.1 %all-to-all-start.1 = ((bf16[8,8,768]{2,1,0:T(8,128)(2,1)}), bf16[8,8,768]{2,1,0:T(8,128)(2,1)S(1)}, u32[]{:S(2)}, u32[]{:S(2)}) async-start(bf16[8,8,768]{2,1,0:T(8,128)(2,1)} %bitcast.40), calls=%async_computation.1 | async-start | bytes 196608 | tf_op jit(solution)/shard_map/all_to_all | solution.py:552
  125.0 0.7 copy-start.13
  125.0 0.7 copy-start.14
  125.0 0.7 copy-start.15
  132.0 0.6 copy-start.12
where the time goes:
time: 139 us; the launch traced here: 138 us
  Pallas kernels  33.9 us (24%)
  waiting for transfers between devices  28.1 us (20%)
  starting transfers between devices  27 us (19%)
  blocking collectives  23.8 us (17%)
  matrix products  11.1 us (8%)
  local copies, waits for them, and re-layouts  9.51 us (7%)
  other arithmetic  4.07 us (3%)
    all_to_all x1, blocking collectives, local(): lax.all_to_all(copies.reshape(128, 24, 128), ('gx', 'gy', 'gz'), 0, 0, ti...  23.8 us
    ppermute x12, starting transfers between devices, plane_shift(): return lax.ppermute(value, ('gx', 'gy'), pairs)  14.8 us
    pallas_call x1, Pallas kernels, local(): pl.pallas_call(sweep_kernel, out_shape=jax.ShapeDtypeStruct((64, STATE),...  13.7 us
    ppermute x6, waiting for transfers between devices, line_shift(): lax.ppermute(value, 'gz', [(s, (s + steps) % N_GZ) for s in range(N_GZ)])  13.3 us
    ppermute x12, waiting for transfers between devices, plane_shift(): return lax.ppermute(value, ('gx', 'gy'), pairs)  11.2 us
    dot_general x1, matrix products, to_bf16_dot(): return jnp.dot(left, right, preferred_element_type=F32).astype(BF)  10.6 us
    ppermute x6, starting transfers between devices, line_shift(): lax.ppermute(value, 'gz', [(s, (s + steps) % N_GZ) for s in range(N_GZ)])  8.86 us
    pallas_call x1, Pallas kernels, local(): pl.pallas_call(noise_kernel, out_shape=jax.ShapeDtypeStruct((N_GZ * 64, N...  7.36 us
  transfers between devices with their start and end apart: 19, of which 5 were waited for; matrix products, arithmetic and copies ran while one was open for 15% of the time, Pallas kernels for 17%

commit v1 on v0

--- a/solution.py
+++ b/solution.py
@@ -31,6 +31,7 @@
 PLANES = STATE // 128
 FACE_COLS = 352
 PARTS = 8
+DEPTH = 2048
 SLOTS = SPAN_Y + SPAN_X - 1 + SPAN_Z - 1 + 14
 
 BF = jnp.bfloat16
@@ -178,7 +179,7 @@
     holder = lax.rem(x + 1, 4)
 
     def load(chunk, ref, start, target, count):
-        span = pl.ds(chunk * 1024, 1024)
+        span = pl.ds(chunk * DEPTH, DEPTH)
         pltpu.make_async_copy(
             ref.at[pl.ds(start, count), span],
             factors.at[chunk, pl.ds(target, count)],
@@ -188,13 +189,13 @@
     def load_rows(chunk):
         for back in range(N_GZ):
             pltpu.make_async_copy(
-                row_refs[back].at[:, pl.ds(chunk * 1024, 1024)],
+                row_refs[back].at[:, pl.ds(chunk * DEPTH, DEPTH)],
                 rows.at[chunk, back],
                 sem_rows.at[chunk],
             ).start()
 
     def load_all(first_refs, second_refs):
-        for chunk in range(4):
+        for chunk in range(CELLS // DEPTH):
             load_rows(chunk)
             load_chunk(functools.partial(load, chunk), first_refs, second_refs)
 
@@ -219,12 +220,12 @@
 
     by_core(core, piece_refs, load_all)
     product = jnp.zeros((N_GZ * 64, FACE_COLS), F32)
-    for chunk in range(4):
+    for chunk in range(CELLS // DEPTH):
         row_block, factor_block = rows.at[chunk], factors.at[chunk]
         pltpu.make_async_copy(row_block, row_block, sem_rows.at[chunk]).wait()
         pltpu.make_async_copy(factor_block, factor_block, sem_factor.at[chunk]).wait()
         product += lax.dot_general(
-            rows[chunk].reshape(N_GZ * 64, 1024),
+            rows[chunk].reshape(N_GZ * 64, DEPTH),
             factors[chunk],
             (((1,), (1,)), ((), ())),
             preferred_element_type=F32,
@@ -293,7 +294,7 @@
         pltpu.make_async_copy(own_ref.at[chunk], own_half.at[chunk], sems.at[2 * bx]).wait()
         pltpu.make_async_copy(other_ref.at[chunk], other_half.at[chunk], sems.at[2 * bx + 1]).wait()
 
-        @pl.loop(0, N_GY)
+        @pl.loop(0, N_GY, unroll=2)
         def _(by):
             place_block(bx, by)
 
@@ -354,6 +355,11 @@
             start = (g // 4 * 2 + c) * 1024 + g % 4 * 256
             values = total[g * 64 : (g + 1) * 64, c * 256 : (c + 1) * 256]
             out[:, start : start + 256] = values.astype(BF)
+
+
+def swap_kernel(out):
+    target, source = iota((64, 64), 0), iota((64, 64), 1)
+    out[...] = one_hot(source == (target & 7) * 8 + (target >> 3))
 
 
 def final_kernel(faces, swap_rows, kriging, noise, out, weights, values, loads, stores):
@@ -475,9 +481,13 @@
     row_order = one_hot(iota((256, 256), 1) == jnp.asarray(row_table())[late][:, None])
     spread = one_hot(iota((N_GZ, 128, 512), 2) == spread_places[:, :, None])
     reorder = one_hot(state_rows[:, None] == iota((STATE, STATE), 1))
-    swap_rows = one_hot(
-        iota((64, 64), 1) == jnp.asarray([(r % 8) * 8 + r // 8 for r in range(64)])[:, None]
-    )
+    swap_rows = pl.pallas_call(
+        swap_kernel,
+        out_shape=jax.ShapeDtypeStruct((64, 64), BF),
+        out_specs=vmem,
+        compiler_params=pltpu.CompilerParams(vmem_limit_bytes=67043328),
+        name="swap_rows",
+    )()
     to_state = one_hot(iota((CELLS, STATE), 0) == jnp.asarray(STATE_CELLS)[None, :])
     step = to_bf16_dot(reorder, to_bf16_dot(kriging_late, to_state))
 
@@ -488,7 +498,8 @@
         (held[1], select, row_order, spread, step, reorder, place)
     )
     pieces = held + [plane_shift(line, 0, 0, 1)]
-    pieces += [plane_shift(piece, 0, 0, 1) for piece in held[1:]]
+    for d in (1, 2, 3):
+        pieces.append(plane_shift(held[d], 0, 0, 1))
 
     copies = pl.pallas_call(
         face_kernel,
@@ -496,11 +507,11 @@
         in_specs=[smem, vmem, vmem] + [anywhere] * 12,
         out_specs=anywhere,
         scratch_shapes=[
-            pltpu.VMEM((4, N_GZ, 64, 1024), BF),
-            pltpu.VMEM((4, FACE_COLS, 1024), BF),
+            pltpu.VMEM((CELLS // DEPTH, N_GZ, 64, DEPTH), BF),
+            pltpu.VMEM((CELLS // DEPTH, FACE_COLS, DEPTH), BF),
             pltpu.VMEM((BX, ENS, 24, 128), BF),
-            pltpu.SemaphoreType.DMA((4,)),
-            pltpu.SemaphoreType.DMA((4,)),
+            pltpu.SemaphoreType.DMA((CELLS // DEPTH,)),
+            pltpu.SemaphoreType.DMA((CELLS // DEPTH,)),
             pltpu.SemaphoreType.DMA((N_GX // 2 * N_GZ,)),
         ],
         compiler_params=pltpu.CompilerParams(vmem_limit_bytes=16 << 20),
@@ -558,6 +569,7 @@
         out_shape=jax.ShapeDtypeStruct((TILES * ENS, CELLS), BF),
         in_specs=[smem] + [vmem] * 5,
         out_specs=vmem,
+        compiler_params=pltpu.CompilerParams(vmem_limit_bytes=67043328),
         name="natural",
     )(place, *home, spread)
 

time: 139 us -> 138 us (level)
  local copies, waits for them, and re-layouts: 9.51 us -> 6.81 us
  waiting for transfers between devices: 28.1 us -> 29.8 us
    unnamed x42 -> x32, local copies, waits for them, and re-layouts: 3.72 us -> 0.98 us
    convert_element_type x5 -> x4, other arithmetic: 3.23 us -> 2.56 us  [one_hot(): return condition.astype(BF)]
  transfers between devices with their start and end apart: 19 -> 19, of which waited for: 5 -> 5; matrix products, arithmetic and copies ran while one was open for 15% -> 14% of each run, Pallas kernels for 17% -> 17%
where the time goes in v1:
time: 138 us
  Pallas kernels  33.4 us (24%)
  waiting for transfers between devices  29.8 us (22%)
  starting transfers between devices  27.7 us (20%)
  blocking collectives  23.8 us (17%)
  matrix products  12.3 us (9%)
  local copies, waits for them, and re-layouts  6.81 us (5%)
  other arithmetic  3.4 us (2%)
    all_to_all x1, blocking collectives, local(): lax.all_to_all(copies.reshape(128, 24, 128), ('gx', 'gy', 'gz'), 0, 0, ti...  23.8 us
    ppermute x12, starting transfers between devices, plane_shift(): return lax.ppermute(value, ('gx', 'gy'), pairs)  14.8 us
    ppermute x6, waiting for transfers between devices, line_shift(): lax.ppermute(value, 'gz', [(s, (s + steps) % N_GZ) for s in range(N_GZ)])  13.3 us
    pallas_call x1, Pallas kernels, local(): pl.pallas_call(sweep_kernel, out_shape=jax.ShapeDtypeStruct((64, STATE),...  12.6 us
    ppermute x12, waiting for transfers between devices, plane_shift(): return lax.ppermute(value, ('gx', 'gy'), pairs)  12.2 us
    dot_general x1, matrix products, to_bf16_dot(): return jnp.dot(left, right, preferred_element_type=F32).astype(BF)  10.6 us
    ppermute x6, starting transfers between devices, line_shift(): lax.ppermute(value, 'gz', [(s, (s + steps) % N_GZ) for s in range(N_GZ)])  8.86 us
    pallas_call x1, Pallas kernels, local(): pl.pallas_call(noise_kernel, out_shape=jax.ShapeDtypeStruct((N_GZ * 64, N...  7.41 us
  transfers between devices with their start and end apart: 19, of which 5 were waited for; matrix products, arithmetic and copies ran while one was open for 14% of the time, Pallas kernels for 17%

profile of v1, /device:TPU:16, one launch (start us, length us, event | category | flops | bytes accessed | tf_op | source)
XLA Modules:
  0.0 137.7 jit_solution(1666328413730099131)
XLA Ops:
  0.0 0.7 fusion.14
  0.7 1.7 %convolution_convert_fusion = bf16[32,4096]{1,0:T(8,128)(2,1)S(1)} fusion(bf16[4096,128]{1,0:T(8,128)(2,1)} %param.10, s32[32]{0:T(128)S(1)} %fusion.14), kind=kOutput, calls=%fused_computation.4 | convolution fusion | flops 33689600 | bytes 1310848 | tf_op jit(solution)/shard_map/dot_general | solution.py:452
  2.4 0.0 copy-start.14
  2.4 0.1 collective-permute-start
  2.5 0.7 fusion.15
  3.2 1.6 %gather_fusion = bf16[8,8,4096]{2,1,0:T(8,128)(2,1)S(1)} fusion(bf16[8,8,4096]{2,1,0:T(8,128)(2,1)} %bitcast.38, s32[1024]{0:T(1024)S(1)} %pad_clamp_fusion), kind=kCustom, calls=%fused_computation | custom fusion | bytes 1048608 | tf_op jit(solution)/shard_map/gather | solution.py:465
  4.8 1.4 collective-permute-start.5
  6.2 0.6 collective-permute-start.6
  6.8 0.0 collective-permute-done
  6.9 3.1 %collective-permute-start.1 = (bf16[2,16,4096]{2,1,0:T(8,128)(2,1)S(1)}, bf16[2,16,4096]{2,1,0:T(8,128)(2,1)S(1)}, u32[]{:S(2)}, u32[]{:S(2)}) collective-permute-start(bf16[2,16,4096]{2,1,0:T(8,128)(2,1)S(1)} %pad_maximum_fusion), channel_id=1, source_target_pairs={{0,16},{4,20},{8,24},{12,28},{16,0},{20,4},{24,8},{28,12},{32,36},... | collective-permute-start | bytes 786440 | tf_op jit(solution)/shard_map/ppermute | solution.py:100
  10.0 0.1 pad_add_fusion.place
  10.1 0.6 collective-permute-start.2
  10.7 2.6 %collective-permute-start.3 = (bf16[2,16,4096]{2,1,0:T(8,128)(2,1)S(1)}, bf16[2,16,4096]{2,1,0:T(8,128)(2,1)S(1)}, u32[]{:S(2)}, u32[]{:S(2)}) collective-permute-start(bf16[2,16,4096]{2,1,0:T(8,128)(2,1)S(1)} %pad_maximum_fusion), channel_id=1, source_target_pairs={{0,24},{4,28},{8,0},{12,4},{16,8},{20,12},{24,16},{28,20},{32,100}... | collective-permute-start | bytes 786440 | tf_op jit(solution)/shard_map/ppermute | solution.py:100
  13.4 1.5 %collective-permute-done.1 = bf16[2,16,4096]{2,1,0:T(8,128)(2,1)S(1)} collective-permute-done((bf16[2,16,4096]{2,1,0:T(8,128)(2,1)S(1)}, bf16[2,16,4096]{2,1,0:T(8,128)(2,1)S(1)}, u32[]{:S(2)}, u32[]{:S(2)}) %collective-permute-start.1) | collective-permute-done | bytes 262176 | tf_op jit(solution)/shard_map/ppermute | solution.py:100
  14.9 2.8 %collective-permute-done.2 = bf16[2,16,4096]{2,1,0:T(8,128)(2,1)S(1)} collective-permute-done((bf16[2,16,4096]{2,1,0:T(8,128)(2,1)S(1)}, bf16[2,16,4096]{2,1,0:T(8,128)(2,1)S(1)}, u32[]{:S(2)}, u32[]{:S(2)}) %collective-permute-start.2) | collective-permute-done | bytes 262176 | tf_op jit(solution)/shard_map/ppermute | solution.py:100
  17.8 0.0 collective-permute-done.3
  17.8 0.0 copy-start
  17.8 2.0 %collective-permute-start.4 = (bf16[128,4096]{1,0:T(8,128)(2,1)S(1)}, bf16[128,4096]{1,0:T(8,128)(2,1)S(1)}, u32[]{:S(2)}, u32[]{:S(2)}) collective-permute-start(bf16[128,4096]{1,0:T(8,128)(2,1)S(1)} %bitcast.26), channel_id=1, source_target_pairs={{0,64},{4,68},{8,72},{12,76},{16,80},{20,84},{24,88},{28,92},{32,4... | collective-permute-start | bytes 3145736 | tf_op jit(solution)/shard_map/ppermute | solution.py:100
  19.8 3.6 %collective-permute-start.8 = (bf16[128,4096]{1,0:T(8,128)(2,1)S(1)}, bf16[128,4096]{1,0:T(8,128)(2,1)}, u32[]{:S(2)}, u32[]{:S(2)}) collective-permute-start(bf16[128,4096]{1,0:T(8,128)(2,1)S(1)} %bitcast.27), channel_id=1, source_target_pairs={{0,4},{4,0},{8,12},{12,8},{16,20},{20,16},{24,28},{28,24},{32,48},... | collective-permute-start | bytes 3145736 | tf_op jit(solution)/shard_map/ppermute | solution.py:100
  23.4 1.0 collective-permute-start.9
  24.4 0.0 copy-done.14
  24.4 10.6 %fusion.4.step_ref = bf16[768,768]{1,0:T(8,128)(2,1)} fusion(s32[768]{0:T(1024)S(1)} %copy-done.12, bf16[768,4096]{1,0:T(8,128)(2,1)} %kriging.1, s32[768]{0:T(1024)S(1)} %copy-done.14), kind=kOutput, calls=%fused_computation.8 | convolution fusion | flops 5742723072 | bytes 7477248 | tf_op jit(solution)/shard_map/dot_general | solution.py:89
  35.0 0.9 dynamic-slice_reduce_fusion
  35.9 0.7 constant_dynamic-slice_fusion
  36.6 0.2 fusion.11.select
  36.8 0.1 fusion.12.row_order
  36.9 1.0 fusion.7.spread
  37.9 1.3 fusion.2.reorder_ref
  39.2 0.0 collective-permute-done.4.refs_5_
  39.2 0.0 collective-permute-start.10
  39.2 0.0 collective-permute-done.5.refs_1_
  39.2 0.5 collective-permute-start.11
  39.7 7.8 %collective-permute-done.8.refs_6_ = bf16[128,4096]{1,0:T(8,128)(2,1)} collective-permute-done((bf16[128,4096]{1,0:T(8,128)(2,1)S(1)}, bf16[128,4096]{1,0:T(8,128)(2,1)}, u32[]{:S(2)}, u32[]{:S(2)}) %collective-permute-start.8) | collective-permute-done | bytes 1048608 | tf_op jit(solution)/shard_map/ppermute | solution.py:100
  47.5 0.0 collective-permute-start.12
  47.5 0.0 collective-permute-done.9.refs_7_
  47.5 0.5 collective-permute-start.13
  48.0 0.0 collective-permute-done.6.refs_2_
  48.0 1.1 collective-permute-start.7
  49.1 13.3 %collective-permute-done.7.refs_3_ = bf16[64,4096]{1,0:T(8,128)(2,1)S(1)} collective-permute-done((bf16[64,4096]{1,0:T(8,128)(2,1)S(1)}, bf16[64,4096]{1,0:T(8,128)(2,1)S(1)}, u32[]{:S(2)}, u32[]{:S(2)}) %collective-permute-start.7) | collective-permute-done | bytes 524320 | tf_op jit(solution)/shard_map/ppermute | solution.py:104
  62.4 0.0 collective-permute-done.10.refs_8_
  62.4 0.0 collective-permute-done.11.refs_9_
  62.4 0.0 collective-permute-done.12.refs_10_
  62.4 0.0 collective-permute-done.13.refs_11_
  62.4 0.0 copy-done.1
  62.4 0.0 copy-done.9
  62.5 4.8 %face_part.1 = bf16[2,2,8,4,24,128]{5,4,3,2,1,0:T(8,128)(2,1)S(1)} custom-call(s32[4]{0:T(128)S(1)} %pad_add_fusion.place, bf16[352,256]{1,0:T(8,128)(2,1)S(1)} %fusion.11.select, bf16[256,256]{1,0:T(8,128)(2,1)S(1)} %fusion.12.row_order, bf16[64,4096]{1,0:T(8,128)(2,1)S(1)} %bitcast.35, bf16[64,4096]{1,0:T(8,128)(2,1)S(1)} %collective-permute-done.5.refs_1_, ...), custom_call_target="tpu_custom_call" | custom-call | tf_op jit(solution)/shard_map/face_part/pallas_call | solution.py:504
  67.3 23.8 %all_to_all.10.own_ref = bf16[128,24,128]{2,1,0:T(8,128)(2,1)S(1)} all-to-all(bf16[128,24,128]{2,1,0:T(8,128)(2,1)S(1)} %bitcast.37), channel_id=1, replica_groups=mesh['gx'=4,'gy'=8,'gz'=4] {'gx','gy','gz'}, dimensions={0} | all-to-all | bytes 1572864 | tf_op jit(solution)/shard_map/all_to_all | solution.py:537
  91.1 0.8 collective-permute-start.14
  91.9 7.4 %noise_part.1 = bf16[256,1024]{1,0:T(8,128)(2,1)} custom-call(s32[4]{0:T(128)} %copy-done.9, bf16[64,4096]{1,0:T(8,128)(2,1)} %bitcast.36, bf16[64,4096]{1,0:T(8,128)(2,1)} %copy-done.7, bf16[64,4096]{1,0:T(8,128)(2,1)} %collective-permute-done.6.refs_2_, bf16[64,4096]{1,0:T(8,128)(2,1)} %copy-done.8, bf16[128,4096]{1,0:T(8,128)(2,1)} %bitcast.31, ...), custom_call_target="tpu_custom_call" | custom-call | tf_op jit(solution)/shard_map/noise_part/pallas_call | solution.py:522
  99.3 1.9 %fusion.16 = (bf16[64,1024]{1,0:T(8,128)(2,1)}, bf16[64,1024]{1,0:T(8,128)(2,1)}, bf16[64,1024]{1,0:T(8,128)(2,1)}, bf16[64,1024]{1,0:T(8,128)(2,1)}) fusion(bf16[256,1024]{1,0:T(8,128)(2,1)} %noise_part.1), kind=kLoop, calls=%fused_computation.44 | loop fusion | bytes 1048576 | tf_op jit(solution)/shard_map/slice | solution.py:538
  101.2 2.4 %collective-permute-start.15 = (bf16[64,1024]{1,0:T(8,128)(2,1)}, bf16[64,1024]{1,0:T(8,128)(2,1)}, u32[]{:S(2)}, u32[]{:S(2)}) collective-permute-start(bf16[64,1024]{1,0:T(8,128)(2,1)} %get-tuple-element.42), channel_id=1, source_target_pairs={{0,3},{1,0},{2,1},{3,2},{4,7},{5,4},{6,5},{7,6},{8,11},{9,8},{10,9... | collective-permute-start | bytes 393224 | tf_op jit(solution)/shard_map/ppermute | solution.py:104
  103.6 0.8 collective-permute-start.16
  104.4 2.6 %collective-permute-start.17 = (bf16[64,1024]{1,0:T(8,128)(2,1)}, bf16[64,1024]{1,0:T(8,128)(2,1)}, u32[]{:S(2)}, u32[]{:S(2)}) collective-permute-start(bf16[64,1024]{1,0:T(8,128)(2,1)} %get-tuple-element.40), channel_id=1, source_target_pairs={{0,1},{1,2},{2,3},{3,0},{4,5},{5,6},{6,7},{7,4},{8,9},{9,10},{10,1... | collective-permute-start | bytes 393224 | tf_op jit(solution)/shard_map/ppermute | solution.py:104
  107.0 0.0 collective-permute-done.14.other_ref
  107.0 0.9 copy-done.11
  107.9 12.6 %sweep.1 = bf16[64,768]{1,0:T(8,128)(2,1)} custom-call(s32[4]{0:T(128)} %copy-done.9, bf16[128,24,128]{2,1,0:T(8,128)(2,1)} %copy-done.10, bf16[128,24,128]{2,1,0:T(8,128)(2,1)} %copy-done.11, bf16[768,768]{1,0:T(8,128)(2,1)} %fusion.4.step_ref, bf16[768,768]{1,0:T(8,128)(2,1)} %fusion.2.reorder_ref), custom_call_target="tpu_custom_call" | custom-call | tf_op jit(solution)/shard_map/sweep/pallas_call | solution.py:544
  120.5 4.0 %all-to-all-start.1 = ((bf16[8,8,768]{2,1,0:T(8,128)(2,1)}), bf16[8,8,768]{2,1,0:T(8,128)(2,1)}, u32[]{:S(2)}, u32[]{:S(2)}) async-start(bf16[8,8,768]{2,1,0:T(8,128)(2,1)} %bitcast.39), calls=%async_computation.1 | async-start | bytes 196608 | tf_op jit(solution)/shard_map/all_to_all | solution.py:563
  124.6 0.6 swap_rows.1
  125.2 0.0 collective-permute-done.15.second
  125.2 0.0 collective-permute-done.16.third
  125.2 0.0 collective-permute-done.17.fourth
  125.2 2.8 %natural.1.noise = bf16[64,4096]{1,0:T(8,128)(2,1)} custom-call(s32[4]{0:T(128)} %copy-done.9, bf16[64,1024]{1,0:T(8,128)(2,1)} %get-tuple-element.43.first, bf16[64,1024]{1,0:T(8,128)(2,1)} %collective-permute-done.15.second, bf16[64,1024]{1,0:T(8,128)(2,1)} %collective-permute-done.16.third, bf16[64,1024]{1,0:T(8,128)(2,1)} %collective-permute-done.17.fourth, ...), custom_call_target="tpu_custom_call" | custom-call | tf_op jit(solution)/shard_map/natural/pallas_call | solution.py:567
  128.0 4.3 %all-to-all-done.1 = bf16[8,8,768]{2,1,0:T(8,128)(2,1)} async-done(((bf16[8,8,768]{2,1,0:T(8,128)(2,1)}), bf16[8,8,768]{2,1,0:T(8,128)(2,1)}, u32[]{:S(2)}, u32[]{:S(2)}) %all-to-all-start.1) | async-done | bytes 98336 | tf_op jit(solution)/shard_map/all_to_all | solution.py:563
  132.4 5.1 %evolve.1 = f32[64,4096]{1,0:T(8,128)} custom-call(bf16[64,768]{1,0:T(8,128)(2,1)} %bitcast.15.faces, bf16[64,64]{1,0:T(8,128)(2,1)} %swap_rows.1, bf16[768,4096]{1,0:T(8,128)(2,1)} %kriging.1, bf16[64,4096]{1,0:T(8,128)(2,1)} %natural.1.noise), custom_call_target="tpu_custom_call" | custom-call | tf_op jit(solution)/shard_map/evolve/pallas_call | solution.py:576
  (34 shorter events, 0.2 us)
Async XLA Ops:
  2.4 22.0 %copy-start.12 = (s32[768]{0:T(1024)S(1)}, s32[768]{0:T(1024)}, u32[]{:S(2)}) copy-start(s32[768]{0:T(1024)} %constant.78.clone) | copy-start | bytes 9220
  2.4 22.0 %copy-start.14 = (s32[768]{0:T(1024)S(1)}, s32[768]{0:T(1024)}, u32[]{:S(2)}) copy-start(s32[768]{0:T(1024)} %constant.81.clone) | copy-start | bytes 9220
  2.4 4.4 %collective-permute-start = (bf16[16,4096]{1,0:T(8,128)(2,1)S(1)}, bf16[16,4096]{1,0:T(8,128)(2,1)S(1)}, u32[]{:S(2)}, u32[]{:S(2)}) collective-permute-start(bf16[16,4096]{1,0:T(8,128)(2,1)S(1)} %slice.43), channel_id=1, source_target_pairs={{0,32},{4,36},{8,40},{12,44},{16,48},{20,52},{24,56},{28,60},{32,0... | collective-permute-start | bytes 393224 | tf_op jit(solution)/shard_map/ppermute | solution.py:100
  4.8 57.6 %copy-start.1 = (bf16[8,8,4096]{2,1,0:T(8,128)(2,1)}, bf16[8,8,4096]{2,1,0:T(8,128)(2,1)S(1)}, u32[]{:S(2)}) copy-start(bf16[8,8,4096]{2,1,0:T(8,128)(2,1)S(1)} %gather_fusion) | copy-start | bytes 1572868
  4.8 34.3 %collective-permute-start.5 = (bf16[64,4096]{1,0:T(8,128)(2,1)S(1)}, bf16[64,4096]{1,0:T(8,128)(2,1)S(1)}, u32[]{:S(2)}, u32[]{:S(2)}) collective-permute-start(bf16[64,4096]{1,0:T(8,128)(2,1)S(1)} %bitcast.32), channel_id=1, source_target_pairs={{0,1},{1,2},{2,3},{3,0},{4,5},{5,6},{6,7},{7,4},{8,9},{9,10},{10,1... | collective-permute-start | bytes 1572872 | tf_op jit(solution)/shard_map/ppermute | solution.py:104
  6.2 41.8 %collective-permute-start.6 = (bf16[64,4096]{1,0:T(8,128)(2,1)S(1)}, bf16[64,4096]{1,0:T(8,128)(2,1)}, u32[]{:S(2)}, u32[]{:S(2)}) collective-permute-start(bf16[64,4096]{1,0:T(8,128)(2,1)S(1)} %bitcast.33), channel_id=1, source_target_pairs={{0,2},{1,3},{2,0},{3,1},{4,6},{5,7},{6,4},{7,5},{8,10},{9,11},{10,... | collective-permute-start | bytes 1572872 | tf_op jit(solution)/shard_map/ppermute | solution.py:104
  6.9 8.0 %collective-permute-start.1 = (bf16[2,16,4096]{2,1,0:T(8,128)(2,1)S(1)}, bf16[2,16,4096]{2,1,0:T(8,128)(2,1)S(1)}, u32[]{:S(2)}, u32[]{:S(2)}) collective-permute-start(bf16[2,16,4096]{2,1,0:T(8,128)(2,1)S(1)} %pad_maximum_fusion), channel_id=1, source_target_pairs={{0,16},{4,20},{8,24},{12,28},{16,0},{20,4},{24,8},{28,12},{32,36},... | collective-permute-start | bytes 786440 | tf_op jit(solution)/shard_map/ppermute | solution.py:100
  10.1 52.3 %copy-start.9 = (s32[4]{0:T(128)}, s32[4]{0:T(128)S(1)}, u32[]{:S(2)}) copy-start(s32[4]{0:T(128)S(1)} %pad_add_fusion.place) | copy-start | bytes 52
  10.1 7.6 %collective-permute-start.2 = (bf16[2,16,4096]{2,1,0:T(8,128)(2,1)S(1)}, bf16[2,16,4096]{2,1,0:T(8,128)(2,1)S(1)}, u32[]{:S(2)}, u32[]{:S(2)}) collective-permute-start(bf16[2,16,4096]{2,1,0:T(8,128)(2,1)S(1)} %pad_maximum_fusion), channel_id=1, source_target_pairs={{0,8},{4,12},{8,16},{12,20},{16,24},{20,28},{24,0},{28,4},{32,96},... | collective-permute-start | bytes 786440 | tf_op jit(solution)/shard_map/ppermute | solution.py:100
  10.7 7.0 %collective-permute-start.3 = (bf16[2,16,4096]{2,1,0:T(8,128)(2,1)S(1)}, bf16[2,16,4096]{2,1,0:T(8,128)(2,1)S(1)}, u32[]{:S(2)}, u32[]{:S(2)}) collective-permute-start(bf16[2,16,4096]{2,1,0:T(8,128)(2,1)S(1)} %pad_maximum_fusion), channel_id=1, source_target_pairs={{0,24},{4,28},{8,0},{12,4},{16,8},{20,12},{24,16},{28,20},{32,100}... | collective-permute-start | bytes 786440 | tf_op jit(solution)/shard_map/ppermute | solution.py:100
  17.8 44.6 %copy-start = (bf16[2,64,4096]{2,1,0:T(8,128)(2,1)}, bf16[2,64,4096]{2,1,0:T(8,128)(2,1)S(1)}, u32[]{:S(2)}) copy-start(bf16[2,64,4096]{2,1,0:T(8,128)(2,1)S(1)} %constant_dynamic-update-slice_fusion) | copy-start | bytes 3145732
  17.8 21.3 %collective-permute-start.4 = (bf16[128,4096]{1,0:T(8,128)(2,1)S(1)}, bf16[128,4096]{1,0:T(8,128)(2,1)S(1)}, u32[]{:S(2)}, u32[]{:S(2)}) collective-permute-start(bf16[128,4096]{1,0:T(8,128)(2,1)S(1)} %bitcast.26), channel_id=1, source_target_pairs={{0,64},{4,68},{8,72},{12,76},{16,80},{20,84},{24,88},{28,92},{32,4... | collective-permute-start | bytes 3145736 | tf_op jit(solution)/shard_map/ppermute | solution.py:100
  19.8 27.7 %collective-permute-start.8 = (bf16[128,4096]{1,0:T(8,128)(2,1)S(1)}, bf16[128,4096]{1,0:T(8,128)(2,1)}, u32[]{:S(2)}, u32[]{:S(2)}) collective-permute-start(bf16[128,4096]{1,0:T(8,128)(2,1)S(1)} %bitcast.27), channel_id=1, source_target_pairs={{0,4},{4,0},{8,12},{12,8},{16,20},{20,16},{24,28},{28,24},{32,48},... | collective-permute-start | bytes 3145736 | tf_op jit(solution)/shard_map/ppermute | solution.py:100
  23.4 24.1 %collective-permute-start.9 = (bf16[128,4096]{1,0:T(8,128)(2,1)S(1)}, bf16[128,4096]{1,0:T(8,128)(2,1)}, u32[]{:S(2)}, u32[]{:S(2)}) collective-permute-start(bf16[128,4096]{1,0:T(8,128)(2,1)S(1)} %bitcast.28), channel_id=1, source_target_pairs={{0,68},{4,64},{8,76},{12,72},{16,84},{20,80},{24,92},{28,88},{32,5... | collective-permute-start | bytes 3145736 | tf_op jit(solution)/shard_map/ppermute | solution.py:100
  24.4 12.5 %copy-start.13 = (s32[4,128]{1,0:T(4,128)S(1)}, s32[4,128]{1,0:T(4,128)}, u32[]{:S(2)}) copy-start(s32[4,128]{1,0:T(4,128)} %constant.77.clone) | copy-start | bytes 6148
  39.2 28.1 %copy-start.2 = (bf16[128,4096]{1,0:T(8,128)(2,1)}, bf16[128,4096]{1,0:T(8,128)(2,1)S(1)}, u32[]{:S(2)}) copy-start(bf16[128,4096]{1,0:T(8,128)(2,1)S(1)} %collective-permute-done.4.refs_5_) | copy-start | bytes 3145732
  39.2 23.2 %collective-permute-start.10 = (bf16[128,4096]{1,0:T(8,128)(2,1)S(1)}, bf16[128,4096]{1,0:T(8,128)(2,1)S(1)}, u32[]{:S(2)}, u32[]{:S(2)}) collective-permute-start(bf16[128,4096]{1,0:T(8,128)(2,1)S(1)} %bitcast.29), channel_id=1, source_target_pairs={{0,32},{4,36},{8,40},{12,44},{16,48},{20,52},{24,56},{28,60},{32,0... | collective-permute-start | bytes 3145736 | tf_op jit(solution)/shard_map/ppermute | solution.py:100
  39.2 28.1 %copy-start.7 = (bf16[64,4096]{1,0:T(8,128)(2,1)}, bf16[64,4096]{1,0:T(8,128)(2,1)S(1)}, u32[]{:S(2)}) copy-start(bf16[64,4096]{1,0:T(8,128)(2,1)S(1)} %collective-permute-done.5.refs_1_) | copy-start | bytes 1572868
  39.2 23.2 %collective-permute-start.11 = (bf16[128,4096]{1,0:T(8,128)(2,1)S(1)}, bf16[128,4096]{1,0:T(8,128)(2,1)S(1)}, u32[]{:S(2)}, u32[]{:S(2)}) collective-permute-start(bf16[128,4096]{1,0:T(8,128)(2,1)S(1)} %collective-permute-done.4.refs_5_), channel_id=1, source_target_pairs={{0,32},{4,36},{8,40},{12,44},{16,48},{20,52},{24,56},{28,60},{32,0... | collective-permute-start | bytes 3145736 | tf_op jit(solution)/shard_map/ppermute | solution.py:100
  47.5 14.9 %collective-permute-start.12 = (bf16[128,4096]{1,0:T(8,128)(2,1)}, bf16[128,4096]{1,0:T(8,128)(2,1)S(1)}, u32[]{:S(2)}, u32[]{:S(2)}) collective-permute-start(bf16[128,4096]{1,0:T(8,128)(2,1)} %collective-permute-done.8.refs_6_), channel_id=1, source_target_pairs={{0,32},{4,36},{8,40},{12,44},{16,48},{20,52},{24,56},{28,60},{32,0... | collective-permute-start | bytes 3145736 | tf_op jit(solution)/shard_map/ppermute | solution.py:100
  47.5 14.9 %collective-permute-start.13 = (bf16[128,4096]{1,0:T(8,128)(2,1)}, bf16[128,4096]{1,0:T(8,128)(2,1)S(1)}, u32[]{:S(2)}, u32[]{:S(2)}) collective-permute-start(bf16[128,4096]{1,0:T(8,128)(2,1)} %collective-permute-done.9.refs_7_), channel_id=1, source_target_pairs={{0,32},{4,36},{8,40},{12,44},{16,48},{20,52},{24,56},{28,60},{32,0... | collective-permute-start | bytes 3145736 | tf_op jit(solution)/shard_map/ppermute | solution.py:100
  48.0 14.3 %collective-permute-start.7 = (bf16[64,4096]{1,0:T(8,128)(2,1)S(1)}, bf16[64,4096]{1,0:T(8,128)(2,1)S(1)}, u32[]{:S(2)}, u32[]{:S(2)}) collective-permute-start(bf16[64,4096]{1,0:T(8,128)(2,1)S(1)} %bitcast.34), channel_id=1, source_target_pairs={{0,3},{1,0},{2,1},{3,2},{4,7},{5,4},{6,5},{7,6},{8,11},{9,8},{10,9... | collective-permute-start | bytes 1572872 | tf_op jit(solution)/shard_map/ppermute | solution.py:104
  62.4 4.9 %copy-start.8 = (bf16[64,4096]{1,0:T(8,128)(2,1)}, bf16[64,4096]{1,0:T(8,128)(2,1)S(1)}, u32[]{:S(2)}) copy-start(bf16[64,4096]{1,0:T(8,128)(2,1)S(1)} %collective-permute-done.7.refs_3_) | copy-start | bytes 1572868
  62.4 4.9 %copy-start.3 = (bf16[128,4096]{1,0:T(8,128)(2,1)}, bf16[128,4096]{1,0:T(8,128)(2,1)S(1)}, u32[]{:S(2)}) copy-start(bf16[128,4096]{1,0:T(8,128)(2,1)S(1)} %collective-permute-done.10.refs_8_) | copy-start | bytes 3145732
  62.4 4.9 %copy-start.4 = (bf16[128,4096]{1,0:T(8,128)(2,1)}, bf16[128,4096]{1,0:T(8,128)(2,1)S(1)}, u32[]{:S(2)}) copy-start(bf16[128,4096]{1,0:T(8,128)(2,1)S(1)} %collective-permute-done.11.refs_9_) | copy-start | bytes 3145732
  62.4 4.9 %copy-start.5 = (bf16[128,4096]{1,0:T(8,128)(2,1)}, bf16[128,4096]{1,0:T(8,128)(2,1)S(1)}, u32[]{:S(2)}) copy-start(bf16[128,4096]{1,0:T(8,128)(2,1)S(1)} %collective-permute-done.12.refs_10_) | copy-start | bytes 3145732
  62.4 4.9 %copy-start.6 = (bf16[128,4096]{1,0:T(8,128)(2,1)}, bf16[128,4096]{1,0:T(8,128)(2,1)S(1)}, u32[]{:S(2)}) copy-start(bf16[128,4096]{1,0:T(8,128)(2,1)S(1)} %collective-permute-done.13.refs_11_) | copy-start | bytes 3145732
  91.1 8.2 %copy-start.10 = (bf16[128,24,128]{2,1,0:T(8,128)(2,1)}, bf16[128,24,128]{2,1,0:T(8,128)(2,1)S(1)}, u32[]{:S(2)}) copy-start(bf16[128,24,128]{2,1,0:T(8,128)(2,1)S(1)} %all_to_all.10.own_ref) | copy-start | bytes 2359300
  91.1 15.9 %collective-permute-start.14 = (bf16[128,24,128]{2,1,0:T(8,128)(2,1)S(1)}, bf16[128,24,128]{2,1,0:T(8,128)(2,1)S(1)}, u32[]{:S(2)}, u32[]{:S(2)}) collective-permute-start(bf16[128,24,128]{2,1,0:T(8,128)(2,1)S(1)} %all_to_all.10.own_ref), channel_id=1, source_target_pairs={{0,32},{4,36},{8,40},{12,44},{16,48},{20,52},{24,56},{28,60},{32,0... | collective-permute-start | bytes 2359304 | tf_op jit(solution)/shard_map/ppermute | solution.py:100
  101.2 23.9 %collective-permute-start.15 = (bf16[64,1024]{1,0:T(8,128)(2,1)}, bf16[64,1024]{1,0:T(8,128)(2,1)}, u32[]{:S(2)}, u32[]{:S(2)}) collective-permute-start(bf16[64,1024]{1,0:T(8,128)(2,1)} %get-tuple-element.42), channel_id=1, source_target_pairs={{0,3},{1,0},{2,1},{3,2},{4,7},{5,4},{6,5},{7,6},{8,11},{9,8},{10,9... | collective-permute-start | bytes 393224 | tf_op jit(solution)/shard_map/ppermute | solution.py:104
  103.6 21.6 %collective-permute-start.16 = (bf16[64,1024]{1,0:T(8,128)(2,1)}, bf16[64,1024]{1,0:T(8,128)(2,1)}, u32[]{:S(2)}, u32[]{:S(2)}) collective-permute-start(bf16[64,1024]{1,0:T(8,128)(2,1)} %get-tuple-element.41), channel_id=1, source_target_pairs={{0,2},{1,3},{2,0},{3,1},{4,6},{5,7},{6,4},{7,5},{8,10},{9,11},{10,... | collective-permute-start | bytes 393224 | tf_op jit(solution)/shard_map/ppermute | solution.py:104
  104.4 20.8 %collective-permute-start.17 = (bf16[64,1024]{1,0:T(8,128)(2,1)}, bf16[64,1024]{1,0:T(8,128)(2,1)}, u32[]{:S(2)}, u32[]{:S(2)}) collective-permute-start(bf16[64,1024]{1,0:T(8,128)(2,1)} %get-tuple-element.40), channel_id=1, source_target_pairs={{0,1},{1,2},{2,3},{3,0},{4,5},{5,6},{6,7},{7,4},{8,9},{9,10},{10,1... | collective-permute-start | bytes 393224 | tf_op jit(solution)/shard_map/ppermute | solution.py:104
  107.0 0.9 copy-start.11
  120.5 11.8 %all-to-all-start.1 = ((bf16[8,8,768]{2,1,0:T(8,128)(2,1)}), bf16[8,8,768]{2,1,0:T(8,128)(2,1)}, u32[]{:S(2)}, u32[]{:S(2)}) async-start(bf16[8,8,768]{2,1,0:T(8,128)(2,1)} %bitcast.39), calls=%async_computation.1 | async-start | bytes 196608 | tf_op jit(solution)/shard_map/all_to_all | solution.py:563

commit v2 on v1

--- a/solution.py
+++ b/solution.py
@@ -294,7 +294,7 @@
         pltpu.make_async_copy(own_ref.at[chunk], own_half.at[chunk], sems.at[2 * bx]).wait()
         pltpu.make_async_copy(other_ref.at[chunk], other_half.at[chunk], sems.at[2 * bx + 1]).wait()
 
-        @pl.loop(0, N_GY, unroll=2)
+        @pl.loop(0, N_GY, unroll=8)
         def _(by):
             place_block(bx, by)
 
@@ -498,8 +498,7 @@
         (held[1], select, row_order, spread, step, reorder, place)
     )
     pieces = held + [plane_shift(line, 0, 0, 1)]
-    for d in (1, 2, 3):
-        pieces.append(plane_shift(held[d], 0, 0, 1))
+    pieces += [plane_shift(piece, 0, 0, 1) for piece in held[1:]]
 
     copies = pl.pallas_call(
         face_kernel,

time: 138 us -> 138 us (level)
  no operation moved by 1% of the time
where the time goes in v2:
time: 138 us; the launch traced here: 137 us
  Pallas kernels  32.9 us (24%)
  waiting for transfers between devices  29.8 us (22%)
  starting transfers between devices  27.7 us (20%)
  blocking collectives  23.8 us (17%)
  matrix products  12.3 us (9%)
  local copies, waits for them, and re-layouts  6.81 us (5%)
  other arithmetic  3.4 us (2%)
    all_to_all x1, blocking collectives, local(): lax.all_to_all(copies.reshape(128, 24, 128), ('gx', 'gy', 'gz'), 0, 0, ti...  23.8 us
    ppermute x12, starting transfers between devices, plane_shift(): return lax.ppermute(value, ('gx', 'gy'), pairs)  14.8 us
    ppermute x6, waiting for transfers between devices, line_shift(): lax.ppermute(value, 'gz', [(s, (s + steps) % N_GZ) for s in range(N_GZ)])  13.3 us
    ppermute x12, waiting for transfers between devices, plane_shift(): return lax.ppermute(value, ('gx', 'gy'), pairs)  12.2 us
    pallas_call x1, Pallas kernels, local(): pl.pallas_call(sweep_kernel, out_shape=jax.ShapeDtypeStruct((64, STATE),...  12.1 us
    dot_general x1, matrix products, to_bf16_dot(): return jnp.dot(left, right, preferred_element_type=F32).astype(BF)  10.6 us
    ppermute x6, starting transfers between devices, line_shift(): lax.ppermute(value, 'gz', [(s, (s + steps) % N_GZ) for s in range(N_GZ)])  8.86 us
    pallas_call x1, Pallas kernels, local(): pl.pallas_call(noise_kernel, out_shape=jax.ShapeDtypeStruct((N_GZ * 64, N...  7.41 us
  transfers between devices with their start and end apart: 19, of which 5 were waited for; matrix products, arithmetic and copies ran while one was open for 14% of the time, Pallas kernels for 17%

profile of v2, /device:TPU:16, one launch (start us, length us, event | category | flops | bytes accessed | tf_op | source)
XLA Modules:
  0.0 137.1 jit_solution(10582366972072993945)
XLA Ops:
  0.0 0.7 fusion.14
  0.7 1.7 %convolution_convert_fusion = bf16[32,4096]{1,0:T(8,128)(2,1)S(1)} fusion(bf16[4096,128]{1,0:T(8,128)(2,1)} %param.10, s32[32]{0:T(128)S(1)} %fusion.14), kind=kOutput, calls=%fused_computation.4 | convolution fusion | flops 33689600 | bytes 1310848 | tf_op jit(solution)/shard_map/dot_general | solution.py:452
  2.4 0.0 copy-start.14
  2.4 0.1 collective-permute-start
  2.5 0.7 fusion.15
  3.2 1.6 %gather_fusion = bf16[8,8,4096]{2,1,0:T(8,128)(2,1)S(1)} fusion(bf16[8,8,4096]{2,1,0:T(8,128)(2,1)} %bitcast.38, s32[1024]{0:T(1024)S(1)} %pad_clamp_fusion), kind=kCustom, calls=%fused_computation | custom fusion | bytes 1048608 | tf_op jit(solution)/shard_map/gather | solution.py:465
  4.8 1.4 collective-permute-start.5
  6.2 0.6 collective-permute-start.6
  6.8 0.0 collective-permute-done
  6.9 3.1 %collective-permute-start.1 = (bf16[2,16,4096]{2,1,0:T(8,128)(2,1)S(1)}, bf16[2,16,4096]{2,1,0:T(8,128)(2,1)S(1)}, u32[]{:S(2)}, u32[]{:S(2)}) collective-permute-start(bf16[2,16,4096]{2,1,0:T(8,128)(2,1)S(1)} %pad_maximum_fusion), channel_id=1, source_target_pairs={{0,16},{4,20},{8,24},{12,28},{16,0},{20,4},{24,8},{28,12},{32,36},... | collective-permute-start | bytes 786440 | tf_op jit(solution)/shard_map/ppermute | solution.py:100
  10.0 0.1 pad_add_fusion.place
  10.1 0.6 collective-permute-start.2
  10.7 2.6 %collective-permute-start.3 = (bf16[2,16,4096]{2,1,0:T(8,128)(2,1)S(1)}, bf16[2,16,4096]{2,1,0:T(8,128)(2,1)S(1)}, u32[]{:S(2)}, u32[]{:S(2)}) collective-permute-start(bf16[2,16,4096]{2,1,0:T(8,128)(2,1)S(1)} %pad_maximum_fusion), channel_id=1, source_target_pairs={{0,24},{4,28},{8,0},{12,4},{16,8},{20,12},{24,16},{28,20},{32,100}... | collective-permute-start | bytes 786440 | tf_op jit(solution)/shard_map/ppermute | solution.py:100
  13.4 1.5 %collective-permute-done.1 = bf16[2,16,4096]{2,1,0:T(8,128)(2,1)S(1)} collective-permute-done((bf16[2,16,4096]{2,1,0:T(8,128)(2,1)S(1)}, bf16[2,16,4096]{2,1,0:T(8,128)(2,1)S(1)}, u32[]{:S(2)}, u32[]{:S(2)}) %collective-permute-start.1) | collective-permute-done | bytes 262176 | tf_op jit(solution)/shard_map/ppermute | solution.py:100
  14.9 2.8 %collective-permute-done.2 = bf16[2,16,4096]{2,1,0:T(8,128)(2,1)S(1)} collective-permute-done((bf16[2,16,4096]{2,1,0:T(8,128)(2,1)S(1)}, bf16[2,16,4096]{2,1,0:T(8,128)(2,1)S(1)}, u32[]{:S(2)}, u32[]{:S(2)}) %collective-permute-start.2) | collective-permute-done | bytes 262176 | tf_op jit(solution)/shard_map/ppermute | solution.py:100
  17.8 0.0 collective-permute-done.3
  17.8 0.0 copy-start
  17.8 2.0 %collective-permute-start.4 = (bf16[128,4096]{1,0:T(8,128)(2,1)S(1)}, bf16[128,4096]{1,0:T(8,128)(2,1)S(1)}, u32[]{:S(2)}, u32[]{:S(2)}) collective-permute-start(bf16[128,4096]{1,0:T(8,128)(2,1)S(1)} %bitcast.26), channel_id=1, source_target_pairs={{0,64},{4,68},{8,72},{12,76},{16,80},{20,84},{24,88},{28,92},{32,4... | collective-permute-start | bytes 3145736 | tf_op jit(solution)/shard_map/ppermute | solution.py:100
  19.8 3.6 %collective-permute-start.8 = (bf16[128,4096]{1,0:T(8,128)(2,1)S(1)}, bf16[128,4096]{1,0:T(8,128)(2,1)}, u32[]{:S(2)}, u32[]{:S(2)}) collective-permute-start(bf16[128,4096]{1,0:T(8,128)(2,1)S(1)} %bitcast.27), channel_id=1, source_target_pairs={{0,4},{4,0},{8,12},{12,8},{16,20},{20,16},{24,28},{28,24},{32,48},... | collective-permute-start | bytes 3145736 | tf_op jit(solution)/shard_map/ppermute | solution.py:100
  23.4 1.0 collective-permute-start.9
  24.4 0.0 copy-done.14
  24.4 10.6 %fusion.4.step_ref = bf16[768,768]{1,0:T(8,128)(2,1)} fusion(s32[768]{0:T(1024)S(1)} %copy-done.12, bf16[768,4096]{1,0:T(8,128)(2,1)} %kriging.1, s32[768]{0:T(1024)S(1)} %copy-done.14), kind=kOutput, calls=%fused_computation.8 | convolution fusion | flops 5742723072 | bytes 7477248 | tf_op jit(solution)/shard_map/dot_general | solution.py:89
  35.0 0.9 dynamic-slice_reduce_fusion
  35.9 0.7 constant_dynamic-slice_fusion
  36.6 0.2 fusion.11.select
  36.8 0.1 fusion.12.row_order
  36.9 1.0 fusion.7.spread
  37.9 1.3 fusion.2.reorder_ref
  39.2 0.0 collective-permute-done.4.refs_5_
  39.2 0.0 collective-permute-start.10
  39.2 0.0 collective-permute-done.5.refs_1_
  39.2 0.5 collective-permute-start.11
  39.7 7.8 %collective-permute-done.8.refs_6_ = bf16[128,4096]{1,0:T(8,128)(2,1)} collective-permute-done((bf16[128,4096]{1,0:T(8,128)(2,1)S(1)}, bf16[128,4096]{1,0:T(8,128)(2,1)}, u32[]{:S(2)}, u32[]{:S(2)}) %collective-permute-start.8) | collective-permute-done | bytes 1048608 | tf_op jit(solution)/shard_map/ppermute | solution.py:100
  47.5 0.0 collective-permute-start.12
  47.5 0.0 collective-permute-done.9.refs_7_
  47.5 0.5 collective-permute-start.13
  48.0 0.0 collective-permute-done.6.refs_2_
  48.0 1.1 collective-permute-start.7
  49.1 13.3 %collective-permute-done.7.refs_3_ = bf16[64,4096]{1,0:T(8,128)(2,1)S(1)} collective-permute-done((bf16[64,4096]{1,0:T(8,128)(2,1)S(1)}, bf16[64,4096]{1,0:T(8,128)(2,1)S(1)}, u32[]{:S(2)}, u32[]{:S(2)}) %collective-permute-start.7) | collective-permute-done | bytes 524320 | tf_op jit(solution)/shard_map/ppermute | solution.py:104
  62.4 0.0 collective-permute-done.10.refs_8_
  62.4 0.0 collective-permute-done.11.refs_9_
  62.4 0.0 collective-permute-done.12.refs_10_
  62.4 0.0 collective-permute-done.13.refs_11_
  62.4 0.0 copy-done.1
  62.4 0.0 copy-done.9
  62.5 4.8 %face_part.1 = bf16[2,2,8,4,24,128]{5,4,3,2,1,0:T(8,128)(2,1)S(1)} custom-call(s32[4]{0:T(128)S(1)} %pad_add_fusion.place, bf16[352,256]{1,0:T(8,128)(2,1)S(1)} %fusion.11.select, bf16[256,256]{1,0:T(8,128)(2,1)S(1)} %fusion.12.row_order, bf16[64,4096]{1,0:T(8,128)(2,1)S(1)} %bitcast.35, bf16[64,4096]{1,0:T(8,128)(2,1)S(1)} %collective-permute-done.5.refs_1_, ...), custom_call_target="tpu_custom_call" | custom-call | tf_op jit(solution)/shard_map/face_part/pallas_call | solution.py:503
  67.3 23.8 %all_to_all.10.own_ref = bf16[128,24,128]{2,1,0:T(8,128)(2,1)S(1)} all-to-all(bf16[128,24,128]{2,1,0:T(8,128)(2,1)S(1)} %bitcast.37), channel_id=1, replica_groups=mesh['gx'=4,'gy'=8,'gz'=4] {'gx','gy','gz'}, dimensions={0} | all-to-all | bytes 1572864 | tf_op jit(solution)/shard_map/all_to_all | solution.py:536
  91.1 0.8 collective-permute-start.14
  91.9 7.4 %noise_part.1 = bf16[256,1024]{1,0:T(8,128)(2,1)} custom-call(s32[4]{0:T(128)} %copy-done.9, bf16[64,4096]{1,0:T(8,128)(2,1)} %bitcast.36, bf16[64,4096]{1,0:T(8,128)(2,1)} %copy-done.7, bf16[64,4096]{1,0:T(8,128)(2,1)} %collective-permute-done.6.refs_2_, bf16[64,4096]{1,0:T(8,128)(2,1)} %copy-done.8, bf16[128,4096]{1,0:T(8,128)(2,1)} %bitcast.31, ...), custom_call_target="tpu_custom_call" | custom-call | tf_op jit(solution)/shard_map/noise_part/pallas_call | solution.py:521
  99.3 1.9 %fusion.16 = (bf16[64,1024]{1,0:T(8,128)(2,1)}, bf16[64,1024]{1,0:T(8,128)(2,1)}, bf16[64,1024]{1,0:T(8,128)(2,1)}, bf16[64,1024]{1,0:T(8,128)(2,1)}) fusion(bf16[256,1024]{1,0:T(8,128)(2,1)} %noise_part.1), kind=kLoop, calls=%fused_computation.44 | loop fusion | bytes 1048576 | tf_op jit(solution)/shard_map/slice | solution.py:537
  101.2 2.4 %collective-permute-start.15 = (bf16[64,1024]{1,0:T(8,128)(2,1)}, bf16[64,1024]{1,0:T(8,128)(2,1)}, u32[]{:S(2)}, u32[]{:S(2)}) collective-permute-start(bf16[64,1024]{1,0:T(8,128)(2,1)} %get-tuple-element.42), channel_id=1, source_target_pairs={{0,3},{1,0},{2,1},{3,2},{4,7},{5,4},{6,5},{7,6},{8,11},{9,8},{10,9... | collective-permute-start | bytes 393224 | tf_op jit(solution)/shard_map/ppermute | solution.py:104
  103.6 0.8 collective-permute-start.16
  104.4 2.6 %collective-permute-start.17 = (bf16[64,1024]{1,0:T(8,128)(2,1)}, bf16[64,1024]{1,0:T(8,128)(2,1)}, u32[]{:S(2)}, u32[]{:S(2)}) collective-permute-start(bf16[64,1024]{1,0:T(8,128)(2,1)} %get-tuple-element.40), channel_id=1, source_target_pairs={{0,1},{1,2},{2,3},{3,0},{4,5},{5,6},{6,7},{7,4},{8,9},{9,10},{10,1... | collective-permute-start | bytes 393224 | tf_op jit(solution)/shard_map/ppermute | solution.py:104
  107.0 0.0 collective-permute-done.14.other_ref
  107.0 0.9 copy-done.11
  107.9 12.1 %sweep.1 = bf16[64,768]{1,0:T(8,128)(2,1)} custom-call(s32[4]{0:T(128)} %copy-done.9, bf16[128,24,128]{2,1,0:T(8,128)(2,1)} %copy-done.10, bf16[128,24,128]{2,1,0:T(8,128)(2,1)} %copy-done.11, bf16[768,768]{1,0:T(8,128)(2,1)} %fusion.4.step_ref, bf16[768,768]{1,0:T(8,128)(2,1)} %fusion.2.reorder_ref), custom_call_target="tpu_custom_call" | custom-call | tf_op jit(solution)/shard_map/sweep/pallas_call | solution.py:543
  120.0 4.0 %all-to-all-start.1 = ((bf16[8,8,768]{2,1,0:T(8,128)(2,1)}), bf16[8,8,768]{2,1,0:T(8,128)(2,1)}, u32[]{:S(2)}, u32[]{:S(2)}) async-start(bf16[8,8,768]{2,1,0:T(8,128)(2,1)} %bitcast.39), calls=%async_computation.1 | async-start | bytes 196608 | tf_op jit(solution)/shard_map/all_to_all | solution.py:562
  124.0 0.6 swap_rows.1
  124.6 0.0 collective-permute-done.15.second
  124.6 0.0 collective-permute-done.16.third
  124.6 0.0 collective-permute-done.17.fourth
  124.6 2.8 %natural.1.noise = bf16[64,4096]{1,0:T(8,128)(2,1)} custom-call(s32[4]{0:T(128)} %copy-done.9, bf16[64,1024]{1,0:T(8,128)(2,1)} %get-tuple-element.43.first, bf16[64,1024]{1,0:T(8,128)(2,1)} %collective-permute-done.15.second, bf16[64,1024]{1,0:T(8,128)(2,1)} %collective-permute-done.16.third, bf16[64,1024]{1,0:T(8,128)(2,1)} %collective-permute-done.17.fourth, ...), custom_call_target="tpu_custom_call" | custom-call | tf_op jit(solution)/shard_map/natural/pallas_call | solution.py:566
  127.5 4.4 %all-to-all-done.1 = bf16[8,8,768]{2,1,0:T(8,128)(2,1)} async-done(((bf16[8,8,768]{2,1,0:T(8,128)(2,1)}), bf16[8,8,768]{2,1,0:T(8,128)(2,1)}, u32[]{:S(2)}, u32[]{:S(2)}) %all-to-all-start.1) | async-done | bytes 98336 | tf_op jit(solution)/shard_map/all_to_all | solution.py:562
  131.8 5.1 %evolve.1 = f32[64,4096]{1,0:T(8,128)} custom-call(bf16[64,768]{1,0:T(8,128)(2,1)} %bitcast.15.faces, bf16[64,64]{1,0:T(8,128)(2,1)} %swap_rows.1, bf16[768,4096]{1,0:T(8,128)(2,1)} %kriging.1, bf16[64,4096]{1,0:T(8,128)(2,1)} %natural.1.noise), custom_call_target="tpu_custom_call" | custom-call | tf_op jit(solution)/shard_map/evolve/pallas_call | solution.py:575
  (34 shorter events, 0.2 us)
Async XLA Ops:
  2.4 22.0 %copy-start.12 = (s32[768]{0:T(1024)S(1)}, s32[768]{0:T(1024)}, u32[]{:S(2)}) copy-start(s32[768]{0:T(1024)} %constant.78.clone) | copy-start | bytes 9220
  2.4 22.0 %copy-start.14 = (s32[768]{0:T(1024)S(1)}, s32[768]{0:T(1024)}, u32[]{:S(2)}) copy-start(s32[768]{0:T(1024)} %constant.81.clone) | copy-start | bytes 9220
  2.4 4.4 %collective-permute-start = (bf16[16,4096]{1,0:T(8,128)(2,1)S(1)}, bf16[16,4096]{1,0:T(8,128)(2,1)S(1)}, u32[]{:S(2)}, u32[]{:S(2)}) collective-permute-start(bf16[16,4096]{1,0:T(8,128)(2,1)S(1)} %slice.43), channel_id=1, source_target_pairs={{0,32},{4,36},{8,40},{12,44},{16,48},{20,52},{24,56},{28,60},{32,0... | collective-permute-start | bytes 393224 | tf_op jit(solution)/shard_map/ppermute | solution.py:100
  4.8 57.6 %copy-start.1 = (bf16[8,8,4096]{2,1,0:T(8,128)(2,1)}, bf16[8,8,4096]{2,1,0:T(8,128)(2,1)S(1)}, u32[]{:S(2)}) copy-start(bf16[8,8,4096]{2,1,0:T(8,128)(2,1)S(1)} %gather_fusion) | copy-start | bytes 1572868
  4.8 34.3 %collective-permute-start.5 = (bf16[64,4096]{1,0:T(8,128)(2,1)S(1)}, bf16[64,4096]{1,0:T(8,128)(2,1)S(1)}, u32[]{:S(2)}, u32[]{:S(2)}) collective-permute-start(bf16[64,4096]{1,0:T(8,128)(2,1)S(1)} %bitcast.32), channel_id=1, source_target_pairs={{0,1},{1,2},{2,3},{3,0},{4,5},{5,6},{6,7},{7,4},{8,9},{9,10},{10,1... | collective-permute-start | bytes 1572872 | tf_op jit(solution)/shard_map/ppermute | solution.py:104
  6.2 41.8 %collective-permute-start.6 = (bf16[64,4096]{1,0:T(8,128)(2,1)S(1)}, bf16[64,4096]{1,0:T(8,128)(2,1)}, u32[]{:S(2)}, u32[]{:S(2)}) collective-permute-start(bf16[64,4096]{1,0:T(8,128)(2,1)S(1)} %bitcast.33), channel_id=1, source_target_pairs={{0,2},{1,3},{2,0},{3,1},{4,6},{5,7},{6,4},{7,5},{8,10},{9,11},{10,... | collective-permute-start | bytes 1572872 | tf_op jit(solution)/shard_map/ppermute | solution.py:104
  6.9 8.0 %collective-permute-start.1 = (bf16[2,16,4096]{2,1,0:T(8,128)(2,1)S(1)}, bf16[2,16,4096]{2,1,0:T(8,128)(2,1)S(1)}, u32[]{:S(2)}, u32[]{:S(2)}) collective-permute-start(bf16[2,16,4096]{2,1,0:T(8,128)(2,1)S(1)} %pad_maximum_fusion), channel_id=1, source_target_pairs={{0,16},{4,20},{8,24},{12,28},{16,0},{20,4},{24,8},{28,12},{32,36},... | collective-permute-start | bytes 786440 | tf_op jit(solution)/shard_map/ppermute | solution.py:100
  10.1 52.3 %copy-start.9 = (s32[4]{0:T(128)}, s32[4]{0:T(128)S(1)}, u32[]{:S(2)}) copy-start(s32[4]{0:T(128)S(1)} %pad_add_fusion.place) | copy-start | bytes 52
  10.1 7.6 %collective-permute-start.2 = (bf16[2,16,4096]{2,1,0:T(8,128)(2,1)S(1)}, bf16[2,16,4096]{2,1,0:T(8,128)(2,1)S(1)}, u32[]{:S(2)}, u32[]{:S(2)}) collective-permute-start(bf16[2,16,4096]{2,1,0:T(8,128)(2,1)S(1)} %pad_maximum_fusion), channel_id=1, source_target_pairs={{0,8},{4,12},{8,16},{12,20},{16,24},{20,28},{24,0},{28,4},{32,96},... | collective-permute-start | bytes 786440 | tf_op jit(solution)/shard_map/ppermute | solution.py:100
  10.7 7.0 %collective-permute-start.3 = (bf16[2,16,4096]{2,1,0:T(8,128)(2,1)S(1)}, bf16[2,16,4096]{2,1,0:T(8,128)(2,1)S(1)}, u32[]{:S(2)}, u32[]{:S(2)}) collective-permute-start(bf16[2,16,4096]{2,1,0:T(8,128)(2,1)S(1)} %pad_maximum_fusion), channel_id=1, source_target_pairs={{0,24},{4,28},{8,0},{12,4},{16,8},{20,12},{24,16},{28,20},{32,100}... | collective-permute-start | bytes 786440 | tf_op jit(solution)/shard_map/ppermute | solution.py:100
  17.8 44.6 %copy-start = (bf16[2,64,4096]{2,1,0:T(8,128)(2,1)}, bf16[2,64,4096]{2,1,0:T(8,128)(2,1)S(1)}, u32[]{:S(2)}) copy-start(bf16[2,64,4096]{2,1,0:T(8,128)(2,1)S(1)} %constant_dynamic-update-slice_fusion) | copy-start | bytes 3145732
  17.8 21.3 %collective-permute-start.4 = (bf16[128,4096]{1,0:T(8,128)(2,1)S(1)}, bf16[128,4096]{1,0:T(8,128)(2,1)S(1)}, u32[]{:S(2)}, u32[]{:S(2)}) collective-permute-start(bf16[128,4096]{1,0:T(8,128)(2,1)S(1)} %bitcast.26), channel_id=1, source_target_pairs={{0,64},{4,68},{8,72},{12,76},{16,80},{20,84},{24,88},{28,92},{32,4... | collective-permute-start | bytes 3145736 | tf_op jit(solution)/shard_map/ppermute | solution.py:100
  19.8 27.7 %collective-permute-start.8 = (bf16[128,4096]{1,0:T(8,128)(2,1)S(1)}, bf16[128,4096]{1,0:T(8,128)(2,1)}, u32[]{:S(2)}, u32[]{:S(2)}) collective-permute-start(bf16[128,4096]{1,0:T(8,128)(2,1)S(1)} %bitcast.27), channel_id=1, source_target_pairs={{0,4},{4,0},{8,12},{12,8},{16,20},{20,16},{24,28},{28,24},{32,48},... | collective-permute-start | bytes 3145736 | tf_op jit(solution)/shard_map/ppermute | solution.py:100
  23.4 24.1 %collective-permute-start.9 = (bf16[128,4096]{1,0:T(8,128)(2,1)S(1)}, bf16[128,4096]{1,0:T(8,128)(2,1)}, u32[]{:S(2)}, u32[]{:S(2)}) collective-permute-start(bf16[128,4096]{1,0:T(8,128)(2,1)S(1)} %bitcast.28), channel_id=1, source_target_pairs={{0,68},{4,64},{8,76},{12,72},{16,84},{20,80},{24,92},{28,88},{32,5... | collective-permute-start | bytes 3145736 | tf_op jit(solution)/shard_map/ppermute | solution.py:100
  24.4 12.5 %copy-start.13 = (s32[4,128]{1,0:T(4,128)S(1)}, s32[4,128]{1,0:T(4,128)}, u32[]{:S(2)}) copy-start(s32[4,128]{1,0:T(4,128)} %constant.77.clone) | copy-start | bytes 6148
  39.2 28.1 %copy-start.2 = (bf16[128,4096]{1,0:T(8,128)(2,1)}, bf16[128,4096]{1,0:T(8,128)(2,1)S(1)}, u32[]{:S(2)}) copy-start(bf16[128,4096]{1,0:T(8,128)(2,1)S(1)} %collective-permute-done.4.refs_5_) | copy-start | bytes 3145732
  39.2 23.2 %collective-permute-start.10 = (bf16[128,4096]{1,0:T(8,128)(2,1)S(1)}, bf16[128,4096]{1,0:T(8,128)(2,1)S(1)}, u32[]{:S(2)}, u32[]{:S(2)}) collective-permute-start(bf16[128,4096]{1,0:T(8,128)(2,1)S(1)} %bitcast.29), channel_id=1, source_target_pairs={{0,32},{4,36},{8,40},{12,44},{16,48},{20,52},{24,56},{28,60},{32,0... | collective-permute-start | bytes 3145736 | tf_op jit(solution)/shard_map/ppermute | solution.py:100
  39.2 28.1 %copy-start.7 = (bf16[64,4096]{1,0:T(8,128)(2,1)}, bf16[64,4096]{1,0:T(8,128)(2,1)S(1)}, u32[]{:S(2)}) copy-start(bf16[64,4096]{1,0:T(8,128)(2,1)S(1)} %collective-permute-done.5.refs_1_) | copy-start | bytes 1572868
  39.2 23.2 %collective-permute-start.11 = (bf16[128,4096]{1,0:T(8,128)(2,1)S(1)}, bf16[128,4096]{1,0:T(8,128)(2,1)S(1)}, u32[]{:S(2)}, u32[]{:S(2)}) collective-permute-start(bf16[128,4096]{1,0:T(8,128)(2,1)S(1)} %collective-permute-done.4.refs_5_), channel_id=1, source_target_pairs={{0,32},{4,36},{8,40},{12,44},{16,48},{20,52},{24,56},{28,60},{32,0... | collective-permute-start | bytes 3145736 | tf_op jit(solution)/shard_map/ppermute | solution.py:100
  47.5 14.9 %collective-permute-start.12 = (bf16[128,4096]{1,0:T(8,128)(2,1)}, bf16[128,4096]{1,0:T(8,128)(2,1)S(1)}, u32[]{:S(2)}, u32[]{:S(2)}) collective-permute-start(bf16[128,4096]{1,0:T(8,128)(2,1)} %collective-permute-done.8.refs_6_), channel_id=1, source_target_pairs={{0,32},{4,36},{8,40},{12,44},{16,48},{20,52},{24,56},{28,60},{32,0... | collective-permute-start | bytes 3145736 | tf_op jit(solution)/shard_map/ppermute | solution.py:100
  47.5 14.9 %collective-permute-start.13 = (bf16[128,4096]{1,0:T(8,128)(2,1)}, bf16[128,4096]{1,0:T(8,128)(2,1)S(1)}, u32[]{:S(2)}, u32[]{:S(2)}) collective-permute-start(bf16[128,4096]{1,0:T(8,128)(2,1)} %collective-permute-done.9.refs_7_), channel_id=1, source_target_pairs={{0,32},{4,36},{8,40},{12,44},{16,48},{20,52},{24,56},{28,60},{32,0... | collective-permute-start | bytes 3145736 | tf_op jit(solution)/shard_map/ppermute | solution.py:100
  48.0 14.3 %collective-permute-start.7 = (bf16[64,4096]{1,0:T(8,128)(2,1)S(1)}, bf16[64,4096]{1,0:T(8,128)(2,1)S(1)}, u32[]{:S(2)}, u32[]{:S(2)}) collective-permute-start(bf16[64,4096]{1,0:T(8,128)(2,1)S(1)} %bitcast.34), channel_id=1, source_target_pairs={{0,3},{1,0},{2,1},{3,2},{4,7},{5,4},{6,5},{7,6},{8,11},{9,8},{10,9... | collective-permute-start | bytes 1572872 | tf_op jit(solution)/shard_map/ppermute | solution.py:104
  62.4 4.9 %copy-start.8 = (bf16[64,4096]{1,0:T(8,128)(2,1)}, bf16[64,4096]{1,0:T(8,128)(2,1)S(1)}, u32[]{:S(2)}) copy-start(bf16[64,4096]{1,0:T(8,128)(2,1)S(1)} %collective-permute-done.7.refs_3_) | copy-start | bytes 1572868
  62.4 4.9 %copy-start.3 = (bf16[128,4096]{1,0:T(8,128)(2,1)}, bf16[128,4096]{1,0:T(8,128)(2,1)S(1)}, u32[]{:S(2)}) copy-start(bf16[128,4096]{1,0:T(8,128)(2,1)S(1)} %collective-permute-done.10.refs_8_) | copy-start | bytes 3145732
  62.4 4.9 %copy-start.4 = (bf16[128,4096]{1,0:T(8,128)(2,1)}, bf16[128,4096]{1,0:T(8,128)(2,1)S(1)}, u32[]{:S(2)}) copy-start(bf16[128,4096]{1,0:T(8,128)(2,1)S(1)} %collective-permute-done.11.refs_9_) | copy-start | bytes 3145732
  62.4 4.9 %copy-start.5 = (bf16[128,4096]{1,0:T(8,128)(2,1)}, bf16[128,4096]{1,0:T(8,128)(2,1)S(1)}, u32[]{:S(2)}) copy-start(bf16[128,4096]{1,0:T(8,128)(2,1)S(1)} %collective-permute-done.12.refs_10_) | copy-start | bytes 3145732
  62.4 4.9 %copy-start.6 = (bf16[128,4096]{1,0:T(8,128)(2,1)}, bf16[128,4096]{1,0:T(8,128)(2,1)S(1)}, u32[]{:S(2)}) copy-start(bf16[128,4096]{1,0:T(8,128)(2,1)S(1)} %collective-permute-done.13.refs_11_) | copy-start | bytes 3145732
  91.1 8.2 %copy-start.10 = (bf16[128,24,128]{2,1,0:T(8,128)(2,1)}, bf16[128,24,128]{2,1,0:T(8,128)(2,1)S(1)}, u32[]{:S(2)}) copy-start(bf16[128,24,128]{2,1,0:T(8,128)(2,1)S(1)} %all_to_all.10.own_ref) | copy-start | bytes 2359300
  91.1 15.9 %collective-permute-start.14 = (bf16[128,24,128]{2,1,0:T(8,128)(2,1)S(1)}, bf16[128,24,128]{2,1,0:T(8,128)(2,1)S(1)}, u32[]{:S(2)}, u32[]{:S(2)}) collective-permute-start(bf16[128,24,128]{2,1,0:T(8,128)(2,1)S(1)} %all_to_all.10.own_ref), channel_id=1, source_target_pairs={{0,32},{4,36},{8,40},{12,44},{16,48},{20,52},{24,56},{28,60},{32,0... | collective-permute-start | bytes 2359304 | tf_op jit(solution)/shard_map/ppermute | solution.py:100
  101.2 23.4 %collective-permute-start.15 = (bf16[64,1024]{1,0:T(8,128)(2,1)}, bf16[64,1024]{1,0:T(8,128)(2,1)}, u32[]{:S(2)}, u32[]{:S(2)}) collective-permute-start(bf16[64,1024]{1,0:T(8,128)(2,1)} %get-tuple-element.42), channel_id=1, source_target_pairs={{0,3},{1,0},{2,1},{3,2},{4,7},{5,4},{6,5},{7,6},{8,11},{9,8},{10,9... | collective-permute-start | bytes 393224 | tf_op jit(solution)/shard_map/ppermute | solution.py:104
  103.6 21.1 %collective-permute-start.16 = (bf16[64,1024]{1,0:T(8,128)(2,1)}, bf16[64,1024]{1,0:T(8,128)(2,1)}, u32[]{:S(2)}, u32[]{:S(2)}) collective-permute-start(bf16[64,1024]{1,0:T(8,128)(2,1)} %get-tuple-element.41), channel_id=1, source_target_pairs={{0,2},{1,3},{2,0},{3,1},{4,6},{5,7},{6,4},{7,5},{8,10},{9,11},{10,... | collective-permute-start | bytes 393224 | tf_op jit(solution)/shard_map/ppermute | solution.py:104
  104.4 20.2 %collective-permute-start.17 = (bf16[64,1024]{1,0:T(8,128)(2,1)}, bf16[64,1024]{1,0:T(8,128)(2,1)}, u32[]{:S(2)}, u32[]{:S(2)}) collective-permute-start(bf16[64,1024]{1,0:T(8,128)(2,1)} %get-tuple-element.40), channel_id=1, source_target_pairs={{0,1},{1,2},{2,3},{3,0},{4,5},{5,6},{6,7},{7,4},{8,9},{9,10},{10,1... | collective-permute-start | bytes 393224 | tf_op jit(solution)/shard_map/ppermute | solution.py:104
  107.0 0.9 copy-start.11
  120.0 11.8 %all-to-all-start.1 = ((bf16[8,8,768]{2,1,0:T(8,128)(2,1)}), bf16[8,8,768]{2,1,0:T(8,128)(2,1)}, u32[]{:S(2)}, u32[]{:S(2)}) async-start(bf16[8,8,768]{2,1,0:T(8,128)(2,1)} %bitcast.39), calls=%async_computation.1 | async-start | bytes 196608 | tf_op jit(solution)/shard_map/all_to_all | solution.py:562
